TPU v7x, 256 devices: a whole 4x4x8 slice. The times are simulated.
256 devices in a mesh: gx: 8 (over x, core), gy: 32 (over z, y).
Axes of the slice: x: 4, y: 4, z: 8, core: 2. Of those that a mesh axis runs over, the one named last changes fastest.
Arguments:
- populations: float32 [19, 32, 256, 128], P(None, 'gx', 'gy'), as said below
- wall_speed: float32 [3, 16384], P(None, ('gx', 'gy')), may hold values from -0.15 to 0.15
- adjoint_seed: float32 [19, 32, 256, 128], P(None, 'gx', 'gy'), may hold values from -6 to 6
- link_cell: int32 [4, 262144], P(None, ('gx', 'gy')), may hold values from 0 to 4095, as said below
- link_dir: int32 [4, 262144], P(None, ('gx', 'gy')), may hold values from 1 to 18
- link_node: int32 [4, 262144], P(None, ('gx', 'gy')), may hold values from 0 to 16383, as said below
- live_links: int32 [4, 256], P(None, ('gx', 'gy')), may hold values from 256 to 1024
- node_slot: int32 [16384], replicated, may hold values from 0 to 16383, as said below
Outputs:
- adjoint_start: float32 [19, 32, 256, 128], P(None, 'gx', 'gy')
- wall_gradient: float32 [3, 16384], P(None, ('gx', 'gy'))
Inputs may be any that keep to these rules, and one draw needn't show every extreme that they name: `link_cell`: A link's cell is numbered x slowest and z fastest within its device's brick of 4 x 8 x 128 cells. `link_node`: A link's node has its slot among the 2048 slots of the devices with the same gx index as the link's device. `node_slot`: A permutation; slot s is held by device s // 64 of gx+gy. `populations`: every population is positive.
All inputs are finite; a program needn't handle non-finite values.
Results may differ from a plain program's by a relative error of at most 0.0003.
Values sent between devices are 32-bit elements; how exact they have to be, the bound alone decides.
No kernel may reach another device: no remote copies, remote signals or barrier semaphores. Data moves between devices by JAX's collectives and lax.ppermute only.
A program may use at most 64 MiB of HBM per device.

v0:
```python
import jax
import jax.numpy as jnp
from jax import lax
from jax.experimental import pallas as pl
from jax.experimental.pallas import tpu as pltpu
from jax.sharding import PartitionSpec as P

VELOCITIES = [
    (0, 0, 0),
    (1, 0, 0),
    (-1, 0, 0),
    (0, 1, 0),
    (0, -1, 0),
    (0, 0, 1),
    (0, 0, -1),
    (1, 1, 0),
    (-1, -1, 0),
    (1, -1, 0),
    (-1, 1, 0),
    (1, 0, 1),
    (-1, 0, -1),
    (1, 0, -1),
    (-1, 0, 1),
    (0, 1, 1),
    (0, -1, -1),
    (0, 1, -1),
    (0, -1, 1),
]
WEIGHTS = [1.0 / 3.0] + [1.0 / 18.0] * 6 + [1.0 / 36.0] * 12
OPPOSITE = [0] + [q + 1 if q % 2 else q - 1 for q in range(1, 19)]
OMEGA = 1.6
F32 = jnp.float32
BF16 = jnp.bfloat16
EXACT = lax.Precision.HIGHEST

POP_TILES = 152
SEED_TILES = 76
LIST_TILES = 8
X_TILES = POP_TILES + SEED_TILES + 3 * LIST_TILES
Y_TILES = 38 + 19 + LIST_TILES


def full(shape=None):
    return pl.BlockSpec(memory_space=pltpu.VMEM)


def row_iota(shape):
    return lax.broadcasted_iota(jnp.int32, shape, 0)


def signs(dirs, component):
    out = jnp.zeros(dirs.shape, F32)
    for q in range(1, 19):
        c = VELOCITIES[q][component]
        if c:
            out = jnp.where(dirs == q, float(c), out)
    return out


def low_half(shape):
    return lax.broadcasted_iota(jnp.int32, shape, len(shape) - 2) < 4


def prep_kernel(
    base, pops, seed, wall, cell, dirs, node, live, table, up_msg, down_msg, lists, slots
):
    low = low_half((8, 128))
    pair = row_iota((8, 128)) // 2
    for q in range(19):
        for i in range(2):
            even = pops[q, 2 * i]
            odd = pltpu.roll(pops[q, 2 * i + 1], 4, 0)
            down_msg[2 * q + i] = jnp.where(low, even, odd)
            up_msg[2 * q + i] = jnp.where(low, odd, even)
        down = seed[q, 0]
        up = pltpu.roll(seed[q, 0], 2, 0)
        for x in range(1, 4):
            down = jnp.where(pair == x, pltpu.roll(seed[q, x], 2 * x, 0), down)
            up = jnp.where(pair == x, pltpu.roll(seed[q, x], (2 * x + 2) % 8, 0) if x < 3 else seed[q, x], up)
        down_msg[38 + q] = down
        up_msg[38 + q] = up
    slot_table = table[...]
    high = (slot_table // 128).astype(F32).astype(BF16)
    rest = (slot_table % 128).astype(F32).astype(BF16)
    both = jnp.concatenate([high, rest], axis=0)
    lanes = row_iota((128, 1024))
    lane = lax.broadcasted_iota(jnp.int32, (1, 1024), 1)
    codes, pushes = [], []
    for s in range(4):
        nodes = node[s : s + 1, :]
        hot = jnp.where(lanes == nodes % 128, 1.0, 0.0).astype(BF16)
        picked = jnp.dot(both, hot, preferred_element_type=F32)
        match = lanes == nodes // 128
        slot_high = jnp.sum(jnp.where(match, picked[:128], 0.0), axis=0, keepdims=True)
        slot_rest = jnp.sum(jnp.where(match, picked[128:], 0.0), axis=0, keepdims=True)
        slot = (slot_high * 128.0 + slot_rest).astype(jnp.int32) - base[0]
        slots[s : s + 1, :] = slot
        owner = row_iota((32, 1024)) == slot // 64
        place = jnp.where(row_iota((64, 1024)) == slot % 64, 1.0, 0.0)
        direction = dirs[s : s + 1, :]
        push = jnp.zeros((1, 1024), F32)
        for c in range(3):
            speeds = jnp.dot(
                wall[:, 64 * c : 64 * c + 64], place, precision=EXACT, preferred_element_type=F32
            )
            speed = jnp.sum(jnp.where(owner, speeds, 0.0), axis=0, keepdims=True)
            push = push + signs(direction, c) * speed
        opposite = direction + 1 - 2 * ((direction + 1) % 2)
        code = opposite * 4096 + cell[s : s + 1, :]
        codes.append(jnp.where(lane < live[s : s + 1, :], code, -1).astype(F32))
        pushes.append(push)
    table8 = jnp.concatenate(codes + pushes, axis=0)
    lists[...] = table8
    for t in range(8):
        up_msg[57 + t] = table8[:, 128 * t : 128 * t + 128]
        down_msg[57 + t] = table8[:, 128 * t : 128 * t + 128]


def pack_kernel(pops, seed, from_up, from_down, lists, right_msg, left_msg):
    low = low_half((8, 128))
    sub = row_iota((8, 128))
    for q in range(19):
        for i in range(2):
            up = from_up[2 * q + i]
            down = from_down[2 * q + i]
            even = jnp.where(low, up, down)
            odd = pltpu.roll(jnp.where(low, down, up), 4, 0)
            for x, halo in ((2 * i, even), (2 * i + 1, odd)):
                k = (q * 4 + x) * 2
                own = pops[q, x]
                for msg in (right_msg, left_msg):
                    msg[k] = own
                    msg[k + 1] = halo
        up = from_up[38 + q]
        down = from_down[38 + q]
        for x in range(4):
            halo = widen_two(up, down, x, sub)
            msg = left_msg if x < 2 else right_msg
            k = POP_TILES + (q * 2 + x % 2) * 2
            msg[k] = seed[q, x]
            msg[k + 1] = halo
    k = POP_TILES + SEED_TILES
    for t in range(8):
        for msg in (right_msg, left_msg):
            msg[k + t] = lists[:, 128 * t : 128 * t + 128]
            msg[k + 8 + t] = from_up[57 + t]
            msg[k + 16 + t] = from_down[57 + t]


def widen_two(up, down, x, sub):
    first = up if x == 0 else pltpu.roll(up, 8 - 2 * x, 0)
    last = down if x == 3 else pltpu.roll(down, 6 - 2 * x, 0)
    return jnp.where(sub < 4, first, last)


def onehot(code, rows, iota):
    out = []
    padded = (rows + 15) // 16 * 16
    for start in range(0, padded, 256):
        count = min(256, padded - start)
        wanted = jnp.clip(code - float(start), -1.0, 256.0).astype(BF16)
        out.append(
            jnp.concatenate(
                [
                    jnp.where(
                        iota[:count] == wanted[:, 128 * t : 128 * t + 128],
                        jnp.array(1.0, BF16),
                        jnp.array(0.0, BF16),
                    )
                    for t in range(8)
                ],
                axis=1,
            )
        )
    return out[0] if len(out) == 1 else jnp.concatenate(out, axis=0)


def iota256():
    return row_iota((256, 128)).astype(F32).astype(BF16)


def split_code(code):
    number = code.astype(jnp.int32)
    dead = number < 0
    z = jnp.where(dead, -1, number % 128)
    row = jnp.where(dead, 0, number // 128)
    return dead, row // 32 - 1, (row // 8) % 4, row % 8, z


def scatter_table(code, push, first, count, iota, part):
    dead, lane_q, x, y, z = split_code(code)
    index = lane_q * count + (x - first)
    outside = dead | (x < first) | (x >= first + count)
    if part == "all":
        row, rows = index * 8 + y, 144 * count
    elif part == "low":
        row, rows = index * 4 + y, 72 * count
        outside = outside | (y >= 4)
    else:
        row, rows = (index + 1 - 2 * (index % 2)) * 4 + y - 4, 72 * count
        outside = outside | (y < 4)
    target = onehot(jnp.where(outside, -1, row).astype(F32), rows, iota)
    zcode = z.astype(F32).astype(BF16)
    high = push.astype(BF16)
    mid = (push - high.astype(F32)).astype(BF16)
    last = (push - high.astype(F32) - mid.astype(F32)).astype(BF16)
    zero = jnp.array(0.0, BF16)
    blocks = [[], [], [], []]
    for t in range(8):
        cut = slice(128 * t, 128 * t + 128)
        match = iota[:128] == zcode[:, cut]
        blocks[0].append(jnp.where(match, jnp.array(1.0, BF16), zero))
        for b, piece in zip(blocks[1:], (high, mid, last)):
            b.append(jnp.where(match, piece[:, cut], zero))
    values = jnp.concatenate([jnp.concatenate(b, axis=1) for b in blocks], axis=0)
    dense = lax.dot_general(
        target, values, (((1,), (1,)), ((), ())), preferred_element_type=F32
    )[:rows]
    return dense[:, :128], dense[:, 128:256] + dense[:, 256:384] + dense[:, 384:]


def scatter_columns(lists, s, first, count, iota, n_ref, s_ref, where):
    own, up, down = lists
    n, p = scatter_table(own[s : s + 1, :], own[4 + s : 5 + s, :], first, count, iota, "all")
    at = pl.ds(where, count)
    n_ref[s, :, at, 0:8, :] = n.reshape(18, count, 8, 128)
    s_ref[s, :, at, 0:8, :] = p.reshape(18, count, 8, 128)
    above = scatter_table(up[s : s + 1, :], up[4 + s : 5 + s, :], first, count, iota, "low")
    below = scatter_table(down[s : s + 1, :], down[4 + s : 5 + s, :], first, count, iota, "high")
    shape = (9 * count, 8, 128)
    low = low_half(shape)
    for ref, a, b in zip((n_ref, s_ref), above, below):
        a, b = a.reshape(shape), b.reshape(shape)
        even = jnp.where(low, a, b)
        odd = pltpu.roll(jnp.where(low, b, a), 4, 1)
        halo = jnp.stack([even, odd], axis=1).reshape(18, count, 8, 128)
        ref[s, :, at, 8:16, :] = halo


def read_list(ref, start):
    return jnp.concatenate([ref[start + t] for t in range(8)], axis=1)


def own_links_kernel(lists, from_up, from_down, n_ref, s_ref):
    iota = iota256()
    both = (lists[...], read_list(from_up, 57), read_list(from_down, 57))
    for s in range(4):
        scatter_columns(both, s, 0, 4, iota, n_ref, s_ref, 0)


def shifted(value, cy, cz):
    if cy:
        value = pltpu.roll(value, cy % 16, 0)
    if cz:
        value = pltpu.roll(value, cz % 128, 1)
    return value


def moments(f):
    rho = f[0]
    for q in range(1, 19):
        rho = rho + f[q]
    inverse = 1.0 / rho
    speeds = []
    for c in range(3):
        total = None
        for q in range(1, 19):
            v = VELOCITIES[q][c]
            if v:
                total = (f[q] if v > 0 else -f[q]) if total is None else (total + f[q] if v > 0 else total - f[q])
        speeds.append(total * inverse)
    return rho, speeds


def along(speeds, q):
    total = None
    for c in range(3):
        v = VELOCITIES[q][c]
        if v:
            term = speeds[c] if v > 0 else -speeds[c]
            total = term if total is None else total + term
    return total


def collide_column(f):
    rho, speeds = moments(f)
    rest = 1.0 - 1.5 * (speeds[0] * speeds[0] + speeds[1] * speeds[1] + speeds[2] * speeds[2])
    out = [(1.0 - OMEGA) * f[0] + (OMEGA * WEIGHTS[0]) * rho * rest]
    for q in range(1, 19, 2):
        cu = along(speeds, q)
        scale = (OMEGA * WEIGHTS[q]) * rho
        even = scale * (rest + 4.5 * cu * cu)
        odd = scale * (3.0 * cu)
        out.append((1.0 - OMEGA) * f[q] + (even + odd))
        out.append((1.0 - OMEGA) * f[q + 1] + (even - odd))
    return out, rho


def collide_into(load, start, count, relaxed, density):
    def body(i, carry):
        f = [load(q, i) for q in range(19)]
        g, rho = collide_column(f)
        for q in range(19):
            relaxed[q, start + i] = g[q]
        density[start + i] = rho
        return carry

    lax.fori_loop(0, count, body, 0)


def stream_into(relaxed, density, n_ref, s_ref, s, start, count, out, out_shift):
    def body(i, carry):
        x = start + i
        rho = density[x]
        out[0, x - out_shift] = relaxed[0, x]
        for q in range(1, 19):
            p = OPPOSITE[q]
            cx, cy, cz = VELOCITIES[q]
            moved = shifted(relaxed[q, x - cx], cy, cz)
            bounce = (0.5 * n_ref[s, q - 1, x]) * (relaxed[p, x] - relaxed[q, x])
            push = (6.0 * WEIGHTS[q]) * rho * s_ref[s, q - 1, x]
            out[q, x - out_shift] = moved + (bounce - push)
        return carry

    lax.fori_loop(0, count, body, 0)


def adjoint_column(f, arrived, local, counts, pushes):
    rho, speeds = moments(f)
    b = [arrived[0]]
    direct = None
    for q in range(1, 19):
        p = OPPOSITE[q]
        b.append(
            arrived[q] + 0.5 * (counts[p - 1] * local[p] - counts[q - 1] * local[q])
        )
        term = (6.0 * WEIGHTS[q]) * (pushes[q - 1] * local[q])
        direct = term if direct is None else direct + term
    beta = [WEIGHTS[q] * b[q] for q in range(19)]
    total = beta[0]
    first = [None] * 3
    second = [None] * 3
    for q in range(1, 19, 2):
        plus = beta[q] + beta[q + 1]
        minus = beta[q] - beta[q + 1]
        total = total + plus
        inner = along(speeds, q) * plus
        for c in range(3):
            v = VELOCITIES[q][c]
            if v:
                m = minus if v > 0 else -minus
                k = inner if v > 0 else -inner
                first[c] = m if first[c] is None else first[c] + m
                second[c] = k if second[c] is None else second[c] + k
    square = speeds[0] * speeds[0] + speeds[1] * speeds[1] + speeds[2] * speeds[2]
    curved = speeds[0] * second[0] + speeds[1] * second[1] + speeds[2] * second[2]
    rest = OMEGA * (total - 4.5 * curved + 1.5 * square * total) - direct
    slopes = [
        OMEGA * (3.0 * first[c] + 9.0 * second[c] - 3.0 * speeds[c] * total) for c in range(3)
    ]
    out = [(1.0 - OMEGA) * b[0] + rest]
    for q in range(1, 19, 2):
        cu = along(slopes, q)
        out.append((1.0 - OMEGA) * b[q] + (rest + cu))
        out.append((1.0 - OMEGA) * b[q + 1] + (rest - cu))
    return out, rho


def adjoint_at(load_f, adjoint, x, counts, pushes):
    f = [load_f(q) for q in range(19)]
    local = [adjoint(q, x) for q in range(19)]
    arrived = []
    for q in range(19):
        cx, cy, cz = VELOCITIES[q]
        value = adjoint(q, x + cx) if cx else local[q]
        arrived.append(shifted(value, -cy, -cz))
    out, rho = adjoint_column(
        f, arrived, local, [counts(q) for q in range(18)], [pushes(q) for q in range(18)]
    )
    return out, rho, local


def ext(ref, k):
    return jnp.concatenate([ref[k], ref[k + 1]], axis=0)


def window_kernel(
    right_msg,
    left_msg,
    from_left,
    from_right,
    n_own,
    s_own,
    f1_out,
    n1_out,
    s1_out,
    a2_out,
    up_msg,
    down_msg,
    pull,
    counts,
    pushes,
    relaxed,
    density,
    f2,
    f3,
    a4,
    a3,
    sems,
):
    copies = [
        pltpu.make_async_copy(n_own, counts.at[:, :, 4:8], sems.at[0]),
        pltpu.make_async_copy(s_own, pushes.at[:, :, 4:8], sems.at[1]),
    ]
    for copy in copies:
        copy.start()
    for ref, start in ((from_left, 0), (right_msg, 4), (from_right, 8)):

        def load(q, i, ref=ref):
            return ref[pl.ds((q * 4 + i) * 2, 2)].reshape(16, 128)

        collide_into(load, start, 4, relaxed, density)
    iota = iota256()
    k = POP_TILES + SEED_TILES
    for ref, right in ((from_left, False), (from_right, True)):
        lists = [read_list(ref, k + 8 * i) for i in range(3)]
        for s, count in ((0, 3), (1, 2), (2, 1), (3, 1)):
            first = 0 if right else 4 - count
            where = 8 if right else 4 - count
            scatter_columns(lists, s, first, count, iota, counts, pushes, where)
    for copy in copies:
        copy.wait()
    stream_into(relaxed, density, counts, pushes, 0, 1, 10, f2, 0)
    for q in range(19):
        f1_out[q] = f2[q, 3:9]
    n1_out[...] = counts[1, :, 3:9]
    s1_out[...] = pushes[1, :, 3:9]
    collide_into(lambda q, i: f2[q, 1 + i], 1, 10, relaxed, density)
    stream_into(relaxed, density, counts, pushes, 1, 2, 8, f2, 0)
    collide_into(lambda q, i: f2[q, 2 + i], 2, 8, relaxed, density)
    stream_into(relaxed, density, counts, pushes, 2, 3, 6, f3, 0)
    for q in range(19):
        for x in range(2):
            k = POP_TILES + (q * 2 + x) * 2
            a4[q, 2 + x] = ext(from_left, k)
            a4[q, 4 + x] = ext(left_msg, k)
            a4[q, 6 + x] = ext(right_msg, k)
            a4[q, 8 + x] = ext(from_right, k)

    def third(i, carry):
        x = 3 + i
        out, rho, local = adjoint_at(
            lambda q: f3[q, x],
            lambda q, at: a4[q, at],
            x,
            lambda q: counts[3, q, x],
            lambda q: pushes[3, q, x],
        )
        for q in range(19):
            a3[q, x] = out[q]

        @pl.when((x >= 4) & (x < 8))
        def _():
            for q in range(1, 19):
                pull[0, q - 1, x - 4] = ((-6.0 * WEIGHTS[q]) * rho * local[q])[:8]

        return carry

    lax.fori_loop(0, 6, third, 0)

    def second(i, carry):
        x = 4 + i
        out, rho, local = adjoint_at(
            lambda q: f2[q, x],
            lambda q, at: a3[q, at],
            x,
            lambda q: counts[2, q, x],
            lambda q: pushes[2, q, x],
        )
        for q in range(19):
            a2_out[q, i] = out[q][:8]
        for q in range(1, 19):
            pull[1, q - 1, i] = ((-6.0 * WEIGHTS[q]) * rho * local[q])[:8]
        return carry

    lax.fori_loop(0, 4, second, 0)
    pair = row_iota((8, 128)) // 2
    for q in range(19):
        down = a2_out[q, 0]
        up = pltpu.roll(a2_out[q, 0], 2, 0)
        for x in range(1, 4):
            value = a2_out[q, x]
            down = jnp.where(pair == x, pltpu.roll(value, 2 * x, 0), down)
            up = jnp.where(pair == x, pltpu.roll(value, (2 * x + 2) % 8, 0) if x < 3 else value, up)
        down_msg[q] = down
        up_msg[q] = up


def pack_adjoint_kernel(a2, from_up, from_down, right_msg, left_msg):
    sub = row_iota((8, 128))
    for q in range(19):
        for x in range(4):
            msg = left_msg if x < 2 else right_msg
            k = (q * 2 + x % 2) * 2
            msg[k] = a2[q, x]
            msg[k + 1] = widen_two(from_up[q], from_down[q], x, sub)


def link_gradient(pulls, lists, slots, dirs, steps):
    iota = iota256()
    total = jnp.zeros((32, 192), F32)
    lanes = row_iota((128, 1024))
    for i, s in enumerate(steps):
        code = lists[s : s + 1, :]
        dead, lane_q, x, y, z = split_code(code)
        row = jnp.where(dead, -1, lane_q * 32 + x * 8 + y).astype(F32)
        hot = onehot(row, 576, iota)
        high = pulls[i].astype(BF16)
        rest = (pulls[i] - high.astype(F32)).astype(BF16)
        low = (pulls[i] - high.astype(F32) - rest.astype(F32)).astype(BF16)
        picked = lax.dot_general(
            jnp.concatenate([high, rest, low], axis=1),
            hot,
            (((0,), (0,)), ((), ())),
            preferred_element_type=F32,
        )
        match = lanes == z
        value = jnp.sum(
            jnp.where(match, picked[:128] + picked[128:256] + picked[256:], 0.0),
            axis=0,
            keepdims=True,
        )
        slot = slots[s : s + 1, :]
        direction = dirs[s : s + 1, :]
        owner = jnp.where(row_iota((32, 1024)) == slot // 64, 1.0, 0.0)
        place = row_iota((64, 1024)) == slot % 64
        parts = jnp.concatenate(
            [jnp.where(place, value * signs(direction, c), 0.0) for c in range(3)], axis=0
        )
        total = total + lax.dot_general(
            owner,
            parts,
            (((1,), (1,)), ((), ())),
            precision=EXACT,
            preferred_element_type=F32,
        )
    return total


def late_links_kernel(pull, lists, slots, dirs, out):
    pulls = [pull[i].reshape(576, 128) for i in range(2)]
    out[...] = link_gradient(pulls, lists, slots, dirs, (3, 2))


def start_kernel(
    right_msg,
    left_msg,
    from_left,
    from_right,
    pops,
    f1,
    n1,
    s1,
    n_own,
    s_own,
    late,
    lists,
    slots,
    dirs,
    a0_out,
    grad_out,
    a2,
    a1,
    pull,
):
    for q in range(19):
        for x in range(2):
            k = (q * 2 + x) * 2
            a2[q, x] = ext(from_left, k)
            a2[q, 2 + x] = ext(left_msg, k)
            a2[q, 4 + x] = ext(right_msg, k)
            a2[q, 6 + x] = ext(from_right, k)

    def first(i, carry):
        x = 1 + i
        out, rho, local = adjoint_at(
            lambda q: f1[q, i],
            lambda q, at: a2[q, at],
            x,
            lambda q: n1[q, i],
            lambda q: s1[q, i],
        )
        for q in range(19):
            a1[q, i] = out[q]

        @pl.when((i >= 1) & (i < 5))
        def _():
            for q in range(1, 19):
                pull[0, q - 1, i - 1] = ((-6.0 * WEIGHTS[q]) * rho * local[q])[:8]

        return carry

    lax.fori_loop(0, 6, first, 0)

    def last(i, carry):
        f = [pops[q, i] for q in range(19)]
        local = [a1[q, 1 + i] for q in range(19)]
        arrived = []
        for q in range(19):
            cx, cy, cz = VELOCITIES[q]
            value = a1[q, 1 + i + cx] if cx else local[q]
            arrived.append(shifted(value, -cy, -cz)[:8])
        local = [v[:8] for v in local]
        out, rho = adjoint_column(
            f, arrived, local, [n_own[q, i, 0:8] for q in range(18)], [s_own[q, i, 0:8] for q in range(18)]
        )
        for q in range(19):
            a0_out[q, i] = out[q]
        for q in range(1, 19):
            pull[1, q - 1, i] = (-6.0 * WEIGHTS[q]) * rho * local[q]
        return carry

    lax.fori_loop(0, 4, last, 0)
    pulls = [pull[i].reshape(576, 128) for i in range(2)]
    grad_out[...] = late[...] + link_gradient(pulls, lists, slots, dirs, (1, 0))


def ring(axis, step):
    count = lax.axis_size(axis)
    return [(i, (i + step) % count) for i in range(count)]


def shape(*dims, dtype=F32):
    return jax.ShapeDtypeStruct(dims, dtype)


def cost(flops, bytes_accessed):
    return pl.CostEstimate(flops=flops, bytes_accessed=bytes_accessed, transcendentals=0)


def shards(
    populations, wall_speed, adjoint_seed, link_cell, link_dir, link_node, live_links, node_slot
):
    vmem = full()
    smem = pl.BlockSpec(memory_space=pltpu.SMEM)
    hbm = pl.BlockSpec(memory_space=pl.ANY)
    copies = jnp.broadcast_to(wall_speed.reshape(1, 192), (32, 192))
    wall = lax.all_to_all(copies, "gy", split_axis=0, concat_axis=0, tiled=True)
    base = (lax.axis_index("gx") * 2048).astype(jnp.int32).reshape(1)
    up_msg, down_msg, lists, slots = pl.pallas_call(
        prep_kernel,
        name="prep",
        out_shape=[
            shape(Y_TILES, 8, 128),
            shape(Y_TILES, 8, 128),
            shape(8, 1024),
            shape(4, 1024, dtype=jnp.int32),
        ],
        in_specs=[smem] + [vmem] * 8,
        out_specs=[vmem] * 4,
    )(
        base,
        populations,
        adjoint_seed,
        wall,
        link_cell,
        link_dir,
        link_node,
        live_links,
        node_slot.reshape(128, 128),
    )
    from_down = lax.ppermute(up_msg, "gy", ring("gy", 1))
    from_up = lax.ppermute(down_msg, "gy", ring("gy", -1))
    right_msg, left_msg = pl.pallas_call(
        pack_kernel,
        name="pack",
        out_shape=[shape(X_TILES, 8, 128)] * 2,
        in_specs=[vmem] * 5,
        out_specs=[vmem] * 2,
    )(populations, adjoint_seed, from_up, from_down, lists)
    from_left = lax.ppermute(right_msg, "gx", ring("gx", 1))
    from_right = lax.ppermute(left_msg, "gx", ring("gx", -1))
    n_own, s_own = pl.pallas_call(
        own_links_kernel,
        name="own_links",
        out_shape=[shape(4, 18, 4, 16, 128)] * 2,
        in_specs=[vmem] * 3,
        out_specs=[vmem] * 2,
        cost_estimate=cost(5_000_000_000, 6_000_000),
        compiler_params=pltpu.CompilerParams(vmem_limit_bytes=48 << 20),
    )(lists, from_up, from_down)
    region = pltpu.VMEM((19, 12, 16, 128), F32)
    f1, n1, s1, a2, up_msg, down_msg, pull = pl.pallas_call(
        window_kernel,
        name="window",
        out_shape=[
            shape(19, 6, 16, 128),
            shape(18, 6, 16, 128),
            shape(18, 6, 16, 128),
            shape(19, 4, 8, 128),
            shape(19, 8, 128),
            shape(19, 8, 128),
            shape(2, 18, 4, 8, 128),
        ],
        in_specs=[vmem] * 4 + [hbm] * 2,
        out_specs=[vmem] * 7,
        scratch_shapes=[
            pltpu.VMEM((4, 18, 12, 16, 128), F32),
            pltpu.VMEM((4, 18, 12, 16, 128), F32),
            region,
            pltpu.VMEM((12, 16, 128), F32),
            region,
            region,
            region,
            region,
            pltpu.SemaphoreType.DMA((2,)),
        ],
        compiler_params=pltpu.CompilerParams(vmem_limit_bytes=58 << 20),
    )(right_msg, left_msg, from_left, from_right, n_own, s_own)
    from_down = lax.ppermute(up_msg, "gy", ring("gy", 1))
    from_up = lax.ppermute(down_msg, "gy", ring("gy", -1))
    right_msg, left_msg = pl.pallas_call(
        pack_adjoint_kernel,
        name="pack_adjoint",
        out_shape=[shape(SEED_TILES, 8, 128)] * 2,
        in_specs=[vmem] * 3,
        out_specs=[vmem] * 2,
    )(a2, from_up, from_down)
    from_left = lax.ppermute(right_msg, "gx", ring("gx", 1))
    from_right = lax.ppermute(left_msg, "gx", ring("gx", -1))
    late = pl.pallas_call(
        late_links_kernel,
        name="late_links",
        out_shape=shape(32, 192),
        in_specs=[vmem] * 4,
        out_specs=vmem,
        cost_estimate=cost(2_000_000_000, 2_000_000),
        compiler_params=pltpu.CompilerParams(vmem_limit_bytes=32 << 20),
    )(pull, lists, slots, link_dir)
    adjoint, owned = pl.pallas_call(
        start_kernel,
        name="start",
        out_shape=[shape(19, 4, 8, 128), shape(32, 192)],
        in_specs=[vmem] * 14,
        out_specs=[vmem] * 2,
        scratch_shapes=[
            pltpu.VMEM((19, 8, 16, 128), F32),
            pltpu.VMEM((19, 6, 16, 128), F32),
            pltpu.VMEM((2, 18, 4, 8, 128), F32),
        ],
        compiler_params=pltpu.CompilerParams(vmem_limit_bytes=48 << 20),
    )(
        right_msg,
        left_msg,
        from_left,
        from_right,
        populations,
        f1,
        n1,
        s1,
        n_own[0],
        s_own[0],
        late,
        lists,
        slots,
        link_dir,
    )
    arrived = lax.all_to_all(owned, "gy", split_axis=0, concat_axis=0, tiled=True)
    return (adjoint, arrived.sum(axis=0).reshape(3, 64))


def solution(mesh):
    placed = (
        P(None, "gx", "gy", None),
        P(None, ("gx", "gy")),
        P(None, "gx", "gy", None),
        P(None, ("gx", "gy")),
        P(None, ("gx", "gy")),
        P(None, ("gx", "gy")),
        P(None, ("gx", "gy")),
        P(),
    )
    return jax.shard_map(
        shards,
        mesh=mesh,
        in_specs=placed,
        out_specs=(P(None, "gx", "gy", None), P(None, ("gx", "gy"))),
        check_vma=False,
    )
```

profile of v0, /device:TPU:8, one launch (start us, length us, event | category | flops | bytes accessed | tf_op | source)
XLA Modules:
  0.0 117.8 jit_solution(2359068898583603342)
XLA Ops:
  2.0 11.7 %all-to-all-start = ((f32[32,1,192]{2,1,0:T(1,128)}), f32[32,1,192]{2,1,0:T(1,128)S(1)}, u32[]{:S(2)}, u32[]{:S(2)}) async-start(f32[32,1,192]{2,1,0:T(1,128)} %broadcast_in_dim.8), calls=%async_computation | async-start | bytes 65536 | tf_op jit(solution)/shard_map/all_to_all | solution.py:648
  13.7 1.3 %copy.11.live = s32[4,1]{1,0:T(4,128)} copy(s32[4,1]{0,1:T(1,128)} %param.14) | data formatting | bytes 32 | tf_op args[6]
  15.1 7.3 %all-to-all-done = f32[32,1,192]{2,1,0:T(1,128)S(1)} async-done(((f32[32,1,192]{2,1,0:T(1,128)}), f32[32,1,192]{2,1,0:T(1,128)S(1)}, u32[]{:S(2)}, u32[]{:S(2)}) %all-to-all-start) | async-done | bytes 24608 | tf_op jit(solution)/shard_map/all_to_all | solution.py:648
  23.0 4.9 %prep.1 = (f32[65,8,128]{2,1,0:T(8,128)}, f32[65,8,128]{2,1,0:T(8,128)}, f32[8,1024]{1,0:T(8,128)}, s32[4,1024]{1,0:T(4,128)}) custom-call(s32[1]{0:T(128)} %bitcast.base, f32[19,4,8,128]{3,2,1,0:T(8,128)} %pops.5, f32[19,4,8,128]{3,2,1,0:T(8,128)} %seed.3, f32[32,192]{1,0:T(8,128)} %bitcast.11, s32[4,1024]{1,0:T(4,128)} %cell.1, s32[4,1024]{1,0:T(4,128)} %dirs.5, ...), custom_call_target="tpu_custom_call" | custom-call | tf_op jit(solution)/shard_map/prep/pallas_call | solution.py:650
  27.9 1.4 %collective-permute-start = (f32[65,8,128]{2,1,0:T(8,128)}, f32[65,8,128]{2,1,0:T(8,128)S(1)}, u32[]{:S(2)}, u32[]{:S(2)}) collective-permute-start(f32[65,8,128]{2,1,0:T(8,128)} %get-tuple-element.21), channel_id=1, source_target_pairs={{0,31},{1,0},{2,1},{3,2},{4,3},{5,4},{6,5},{7,6},{8,7},{9,8},{10,9... | collective-permute-start | bytes 798728 | tf_op jit(solution)/shard_map/ppermute | solution.py:673
  29.9 4.9 %collective-permute-done.from_up = f32[65,8,128]{2,1,0:T(8,128)S(1)} collective-permute-done((f32[65,8,128]{2,1,0:T(8,128)}, f32[65,8,128]{2,1,0:T(8,128)S(1)}, u32[]{:S(2)}, u32[]{:S(2)}) %collective-permute-start) | collective-permute-done | bytes 266272 | tf_op jit(solution)/shard_map/ppermute | solution.py:673
  34.8 1.2 collective-permute-done.1.from_down
  36.6 2.7 %pack.1 = (f32[252,8,128]{2,1,0:T(8,128)}, f32[252,8,128]{2,1,0:T(8,128)}) custom-call(f32[19,4,8,128]{3,2,1,0:T(8,128)} %pops.5, f32[19,4,8,128]{3,2,1,0:T(8,128)} %seed.3, f32[65,8,128]{2,1,0:T(8,128)} %copy-done.8, f32[65,8,128]{2,1,0:T(8,128)} %copy-done.10, f32[8,1024]{1,0:T(8,128)} %get-tuple-element.23.lists), custom_call_target="tpu_custom_call" | custom-call | tf_op jit(solution)/shard_map/pack/pallas_call | solution.py:674
  39.4 3.0 %collective-permute-start.3 = (f32[252,8,128]{2,1,0:T(8,128)}, f32[252,8,128]{2,1,0:T(8,128)S(1)}, u32[]{:S(2)}, u32[]{:S(2)}) collective-permute-start(f32[252,8,128]{2,1,0:T(8,128)} %get-tuple-element.25.left_msg), channel_id=1, source_target_pairs={{0,224},{32,0},{64,32},{96,64},{128,96},{160,128},{192,160},{224,1... | collective-permute-start | bytes 3096584 | tf_op jit(solution)/shard_map/ppermute | solution.py:682
  45.0 5.1 %own_links.1 = (f32[4,18,4,16,128]{4,3,2,1,0:T(8,128)S(1)}, f32[4,18,4,16,128]{4,3,2,1,0:T(8,128)S(1)}) custom-call(f32[8,1024]{1,0:T(8,128)S(1)} %copy-done.12, f32[65,8,128]{2,1,0:T(8,128)S(1)} %copy-done.9, f32[65,8,128]{2,1,0:T(8,128)S(1)} %copy-done.11), custom_call_target="tpu_custom_call" | custom-call | flops 5000000000 | bytes 6000000 | tf_op jit(solution)/shard_map/own_links/pallas_call | solution.py:683
  50.1 1.4 %copy-done = f32[4,18,4,16,128]{4,3,2,1,0:T(8,128)} copy-done((f32[4,18,4,16,128]{4,3,2,1,0:T(8,128)}, f32[4,18,4,16,128]{4,3,2,1,0:T(8,128)S(1)}, u32[]{:S(2)}) %copy-start) | copy-done | bytes 2359320
  51.5 1.4 %copy-done.1 = f32[4,18,4,16,128]{4,3,2,1,0:T(8,128)} copy-done((f32[4,18,4,16,128]{4,3,2,1,0:T(8,128)}, f32[4,18,4,16,128]{4,3,2,1,0:T(8,128)S(1)}, u32[]{:S(2)}) %copy-start.1) | copy-done | bytes 2359320
  53.0 1.8 %collective-permute-done.2.from_left = f32[252,8,128]{2,1,0:T(8,128)S(1)} collective-permute-done((f32[252,8,128]{2,1,0:T(8,128)}, f32[252,8,128]{2,1,0:T(8,128)S(1)}, u32[]{:S(2)}, u32[]{:S(2)}) %collective-permute-start.2) | collective-permute-done | bytes 1032224 | tf_op jit(solution)/shard_map/ppermute | solution.py:681
  54.8 1.0 copy-done.17
  56.2 17.9 %window.1 = (f32[19,6,16,128]{3,2,1,0:T(8,128)}, f32[18,6,16,128]{3,2,1,0:T(8,128)}, f32[18,6,16,128]{3,2,1,0:T(8,128)}, f32[19,4,8,128]{3,2,1,0:T(8,128)}, f32[...) custom-call(f32[252,8,128]{2,1,0:T(8,128)} %get-tuple-element.24.right_msg, ...), custom_call_target="tpu_custom_call" | custom-call | tf_op jit(solution)/shard_map/window/pallas_call | solution.py:693
  74.1 4.8 %collective-permute-start.4 = (f32[19,8,128]{2,1,0:T(8,128)}, f32[19,8,128]{2,1,0:T(8,128)S(1)}, u32[]{:S(2)}, u32[]{:S(2)}) collective-permute-start(f32[19,8,128]{2,1,0:T(8,128)} %get-tuple-element.29), channel_id=1, source_target_pairs={{0,31},{1,0},{2,1},{3,2},{4,3},{5,4},{6,5},{7,6},{8,7},{9,8},{10,9... | collective-permute-start | bytes 233480 | tf_op jit(solution)/shard_map/ppermute | solution.py:721
  78.9 2.3 %collective-permute-done.4.from_up = f32[19,8,128]{2,1,0:T(8,128)S(1)} collective-permute-done((f32[19,8,128]{2,1,0:T(8,128)}, f32[19,8,128]{2,1,0:T(8,128)S(1)}, u32[]{:S(2)}, u32[]{:S(2)}) %collective-permute-start.4) | collective-permute-done | bytes 77856 | tf_op jit(solution)/shard_map/ppermute | solution.py:721
  81.3 2.3 %collective-permute-done.5.from_down = f32[19,8,128]{2,1,0:T(8,128)S(1)} collective-permute-done((f32[19,8,128]{2,1,0:T(8,128)}, f32[19,8,128]{2,1,0:T(8,128)S(1)}, u32[]{:S(2)}, u32[]{:S(2)}) %collective-permute-start.5) | collective-permute-done | bytes 77856 | tf_op jit(solution)/shard_map/ppermute | solution.py:720
  84.2 1.9 %pack_adjoint.1 = (f32[76,8,128]{2,1,0:T(8,128)}, f32[76,8,128]{2,1,0:T(8,128)}) custom-call(f32[19,4,8,128]{3,2,1,0:T(8,128)} %get-tuple-element.28.a2, f32[19,8,128]{2,1,0:T(8,128)} %copy-done.19, f32[19,8,128]{2,1,0:T(8,128)} %copy-done.20), custom_call_target="tpu_custom_call" | custom-call | tf_op jit(solution)/shard_map/pack_adjoint/pallas_call | solution.py:722
  86.1 3.0 %collective-permute-start.7 = (f32[76,8,128]{2,1,0:T(8,128)}, f32[76,8,128]{2,1,0:T(8,128)S(1)}, u32[]{:S(2)}, u32[]{:S(2)}) collective-permute-start(f32[76,8,128]{2,1,0:T(8,128)} %get-tuple-element.32.left_msg), channel_id=1, source_target_pairs={{0,224},{32,0},{64,32},{96,64},{128,96},{160,128},{192,160},{224,1... | collective-permute-start | bytes 933896 | tf_op jit(solution)/shard_map/ppermute | solution.py:730
  89.1 1.4 %slice_bitcast_fusion = (f32[18,4,16,128]{3,2,1,0:T(8,128)S(1)}, f32[18,4,16,128]{3,2,1,0:T(8,128)S(1)}) fusion(f32[4,18,4,16,128]{4,3,2,1,0:T(8,128)} %copy-done.1, f32[4,18,4,16,128]{4,3,2,1,0:T(8,128)} %copy-done), kind=kLoop, calls=%fused_computation | loop fusion | bytes 2359296 | tf_op jit(solution)/shard_map/squeeze | solution.py:762
  90.5 4.3 %late_links.1.late = f32[32,192]{1,0:T(8,128)S(1)} custom-call(f32[2,18,4,8,128]{4,3,2,1,0:T(8,128)S(1)} %copy-done.16, f32[8,1024]{1,0:T(8,128)S(1)} %copy-done.13, s32[4,1024]{1,0:T(4,128)S(1)} %copy-done.15, s32[4,1024]{1,0:T(4,128)S(1)} %copy-done.14), custom_call_target="tpu_custom_call" | custom-call | flops 2000000000 | bytes 2000000 | tf_op jit(solution)/shard_map/late_links/pallas_call | solution.py:731
  94.9 5.7 %start.1 = (f32[19,4,8,128]{3,2,1,0:T(8,128)}, f32[32,192]{1,0:T(8,128)S(1)}) custom-call(f32[76,8,128]{2,1,0:T(8,128)S(1)} %copy-done.6, f32[76,8,128]{2,1,0:T(8,128)S(1)} %copy-done.7, f32[76,8,128]{2,1,0:T(8,128)S(1)} %collective-permute-done.6.from_left, f32[76,8,128]{2,1,0:T(8,128)S(1)} %collective-permute-done.7.from_right, ...), custom_call_target="tpu_custom_call" | custom-call | tf_op jit(solution)/shard_map/start/pallas_call | solution.py:740
  100.6 16.5 %all_to_all.17 = f32[32,1,192]{2,1,0:T(1,128)S(1)} all-to-all(f32[32,1,192]{2,1,0:T(1,128)S(1)} %copy.12), channel_id=1, replica_groups=mesh['gx'=8,'gy'=32] {'gy'}, dimensions={0} | all-to-all | bytes 49152 | tf_op jit(solution)/shard_map/all_to_all | solution.py:768
  (52 shorter events, 7.8 us)
Async XLA Ops:
  2.0 20.3 %all-to-all-start = ((f32[32,1,192]{2,1,0:T(1,128)}), f32[32,1,192]{2,1,0:T(1,128)S(1)}, u32[]{:S(2)}, u32[]{:S(2)}) async-start(f32[32,1,192]{2,1,0:T(1,128)} %broadcast_in_dim.8), calls=%async_computation | async-start | bytes 65536 | tf_op jit(solution)/shard_map/all_to_all | solution.py:648
  27.9 6.9 %collective-permute-start = (f32[65,8,128]{2,1,0:T(8,128)}, f32[65,8,128]{2,1,0:T(8,128)S(1)}, u32[]{:S(2)}, u32[]{:S(2)}) collective-permute-start(f32[65,8,128]{2,1,0:T(8,128)} %get-tuple-element.21), channel_id=1, source_target_pairs={{0,31},{1,0},{2,1},{3,2},{4,3},{5,4},{6,5},{7,6},{8,7},{9,8},{10,9... | collective-permute-start | bytes 798728 | tf_op jit(solution)/shard_map/ppermute | solution.py:673
  29.3 6.6 %collective-permute-start.1 = (f32[65,8,128]{2,1,0:T(8,128)}, f32[65,8,128]{2,1,0:T(8,128)S(1)}, u32[]{:S(2)}, u32[]{:S(2)}) collective-permute-start(f32[65,8,128]{2,1,0:T(8,128)} %get-tuple-element.22), channel_id=1, source_target_pairs={{0,1},{1,2},{2,3},{3,4},{4,5},{5,6},{6,7},{7,8},{8,9},{9,10},{10,1... | collective-permute-start | bytes 798728 | tf_op jit(solution)/shard_map/ppermute | solution.py:672
  34.8 1.2 copy-start.8
  39.4 15.5 %collective-permute-start.2 = (f32[252,8,128]{2,1,0:T(8,128)}, f32[252,8,128]{2,1,0:T(8,128)S(1)}, u32[]{:S(2)}, u32[]{:S(2)}) collective-permute-start(f32[252,8,128]{2,1,0:T(8,128)} %get-tuple-element.24.right_msg), channel_id=1, source_target_pairs={{0,32},{32,64},{64,96},{96,128},{128,160},{160,192},{192,224},{224... | collective-permute-start | bytes 3096584 | tf_op jit(solution)/shard_map/ppermute | solution.py:681
  39.4 15.5 %collective-permute-start.3 = (f32[252,8,128]{2,1,0:T(8,128)}, f32[252,8,128]{2,1,0:T(8,128)S(1)}, u32[]{:S(2)}, u32[]{:S(2)}) collective-permute-start(f32[252,8,128]{2,1,0:T(8,128)} %get-tuple-element.25.left_msg), channel_id=1, source_target_pairs={{0,224},{32,0},{64,32},{96,64},{128,96},{160,128},{192,160},{224,1... | collective-permute-start | bytes 3096584 | tf_op jit(solution)/shard_map/ppermute | solution.py:682
  50.1 1.4 %copy-start = (f32[4,18,4,16,128]{4,3,2,1,0:T(8,128)}, f32[4,18,4,16,128]{4,3,2,1,0:T(8,128)S(1)}, u32[]{:S(2)}) copy-start(f32[4,18,4,16,128]{4,3,2,1,0:T(8,128)S(1)} %get-tuple-element.26.n_own) | copy-start | bytes 7077892
  51.5 1.4 %copy-start.1 = (f32[4,18,4,16,128]{4,3,2,1,0:T(8,128)}, f32[4,18,4,16,128]{4,3,2,1,0:T(8,128)S(1)}, u32[]{:S(2)}) copy-start(f32[4,18,4,16,128]{4,3,2,1,0:T(8,128)S(1)} %get-tuple-element.27.s_own) | copy-start | bytes 7077892
  54.8 1.3 %copy-start.18 = (f32[252,8,128]{2,1,0:T(8,128)}, f32[252,8,128]{2,1,0:T(8,128)S(1)}, u32[]{:S(2)}) copy-start(f32[252,8,128]{2,1,0:T(8,128)S(1)} %collective-permute-done.3.from_right) | copy-start | bytes 3096580
  74.1 16.3 %copy-start.13 = (f32[8,1024]{1,0:T(8,128)S(1)}, f32[8,1024]{1,0:T(8,128)}, u32[]{:S(2)}) copy-start(f32[8,1024]{1,0:T(8,128)} %get-tuple-element.23.lists) | copy-start | bytes 98308
  74.1 16.3 %copy-start.14 = (s32[4,1024]{1,0:T(4,128)S(1)}, s32[4,1024]{1,0:T(4,128)}, u32[]{:S(2)}) copy-start(s32[4,1024]{1,0:T(4,128)} %dirs.5) | copy-start | bytes 49156
  74.1 16.3 %copy-start.15 = (s32[4,1024]{1,0:T(4,128)S(1)}, s32[4,1024]{1,0:T(4,128)}, u32[]{:S(2)}) copy-start(s32[4,1024]{1,0:T(4,128)} %get-tuple-element.37.slots) | copy-start | bytes 49156
  74.1 16.3 %copy-start.16 = (f32[2,18,4,8,128]{4,3,2,1,0:T(8,128)S(1)}, f32[2,18,4,8,128]{4,3,2,1,0:T(8,128)}, u32[]{:S(2)}) copy-start(f32[2,18,4,8,128]{4,3,2,1,0:T(8,128)} %get-tuple-element.36.pull) | copy-start | bytes 1769476
  74.1 7.1 %collective-permute-start.4 = (f32[19,8,128]{2,1,0:T(8,128)}, f32[19,8,128]{2,1,0:T(8,128)S(1)}, u32[]{:S(2)}, u32[]{:S(2)}) collective-permute-start(f32[19,8,128]{2,1,0:T(8,128)} %get-tuple-element.29), channel_id=1, source_target_pairs={{0,31},{1,0},{2,1},{3,2},{4,3},{5,4},{6,5},{7,6},{8,7},{9,8},{10,9... | collective-permute-start | bytes 233480 | tf_op jit(solution)/shard_map/ppermute | solution.py:721
  78.9 4.6 %collective-permute-start.5 = (f32[19,8,128]{2,1,0:T(8,128)}, f32[19,8,128]{2,1,0:T(8,128)S(1)}, u32[]{:S(2)}, u32[]{:S(2)}) collective-permute-start(f32[19,8,128]{2,1,0:T(8,128)} %get-tuple-element.30), channel_id=1, source_target_pairs={{0,1},{1,2},{2,3},{3,4},{4,5},{5,6},{6,7},{7,8},{8,9},{9,10},{10,1... | collective-permute-start | bytes 233480 | tf_op jit(solution)/shard_map/ppermute | solution.py:720
  81.3 2.3 %copy-start.19 = (f32[19,8,128]{2,1,0:T(8,128)}, f32[19,8,128]{2,1,0:T(8,128)S(1)}, u32[]{:S(2)}) copy-start(f32[19,8,128]{2,1,0:T(8,128)S(1)} %collective-permute-done.4.from_up) | copy-start | bytes 233476
  86.1 8.7 %collective-permute-start.6 = (f32[76,8,128]{2,1,0:T(8,128)}, f32[76,8,128]{2,1,0:T(8,128)S(1)}, u32[]{:S(2)}, u32[]{:S(2)}) collective-permute-start(f32[76,8,128]{2,1,0:T(8,128)} %get-tuple-element.31.right_msg), channel_id=1, source_target_pairs={{0,32},{32,64},{64,96},{96,128},{128,160},{160,192},{192,224},{224... | collective-permute-start | bytes 933896 | tf_op jit(solution)/shard_map/ppermute | solution.py:729
  86.1 8.7 %collective-permute-start.7 = (f32[76,8,128]{2,1,0:T(8,128)}, f32[76,8,128]{2,1,0:T(8,128)S(1)}, u32[]{:S(2)}, u32[]{:S(2)}) collective-permute-start(f32[76,8,128]{2,1,0:T(8,128)} %get-tuple-element.32.left_msg), channel_id=1, source_target_pairs={{0,224},{32,0},{64,32},{96,64},{128,96},{160,128},{192,160},{224,1... | collective-permute-start | bytes 933896 | tf_op jit(solution)/shard_map/ppermute | solution.py:730
  90.5 4.4 %copy-start.2 = (f32[19,4,8,128]{3,2,1,0:T(8,128)S(1)}, f32[19,4,8,128]{3,2,1,0:T(8,128)}, u32[]{:S(2)}) copy-start(f32[19,4,8,128]{3,2,1,0:T(8,128)} %pops.5) | copy-start | bytes 933892
  90.5 4.4 %copy-start.3 = (f32[19,6,16,128]{3,2,1,0:T(8,128)S(1)}, f32[19,6,16,128]{3,2,1,0:T(8,128)}, u32[]{:S(2)}) copy-start(f32[19,6,16,128]{3,2,1,0:T(8,128)} %get-tuple-element.33.f1) | copy-start | bytes 2801668
  90.5 4.4 %copy-start.4 = (f32[18,6,16,128]{3,2,1,0:T(8,128)S(1)}, f32[18,6,16,128]{3,2,1,0:T(8,128)}, u32[]{:S(2)}) copy-start(f32[18,6,16,128]{3,2,1,0:T(8,128)} %get-tuple-element.34.n1) | copy-start | bytes 2654212
  90.5 4.4 %copy-start.5 = (f32[18,6,16,128]{3,2,1,0:T(8,128)S(1)}, f32[18,6,16,128]{3,2,1,0:T(8,128)}, u32[]{:S(2)}) copy-start(f32[18,6,16,128]{3,2,1,0:T(8,128)} %get-tuple-element.35.s1) | copy-start | bytes 2654212
  90.5 4.4 %copy-start.6 = (f32[76,8,128]{2,1,0:T(8,128)S(1)}, f32[76,8,128]{2,1,0:T(8,128)}, u32[]{:S(2)}) copy-start(f32[76,8,128]{2,1,0:T(8,128)} %get-tuple-element.31.right_msg) | copy-start | bytes 933892
  90.5 4.4 %copy-start.7 = (f32[76,8,128]{2,1,0:T(8,128)S(1)}, f32[76,8,128]{2,1,0:T(8,128)}, u32[]{:S(2)}) copy-start(f32[76,8,128]{2,1,0:T(8,128)} %get-tuple-element.32.left_msg) | copy-start | bytes 933892
  (6 other events, 5.0 us)
where the time goes:
time: 118 us
  Pallas kernels  42.5 us (36%)
  starting transfers between devices  24.4 us (21%)
  waiting for transfers between devices  19.9 us (17%)
  blocking collectives  16.5 us (14%)
  local copies, waits for them, and re-layouts  13.6 us (12%)
    pallas_call x1, Pallas kernels, shards(): pl.pallas_call(window_kernel, name='window', out_shape=[shape(19, 6, 16,...  17.9 us
    all_to_all x1, blocking collectives, shards(): lax.all_to_all(owned, 'gy', split_axis=0, concat_axis=0, tiled=True)  16.5 us
    all_to_all x1, starting transfers between devices, shards(): wall = lax.all_to_all(copies, 'gy', split_axis=0, concat_axis=0, tiled=True)  11.7 us
    unnamed x44, local copies, waits for them, and re-layouts  10.1 us
    all_to_all x1, waiting for transfers between devices, shards(): wall = lax.all_to_all(copies, 'gy', split_axis=0, concat_axis=0, tiled=True)  7.32 us
    ppermute x2, waiting for transfers between devices, shards(): from_up = lax.ppermute(down_msg, 'gy', ring('gy', -1))  7.22 us
    ppermute x2, starting transfers between devices, shards(): from_up = lax.ppermute(down_msg, 'gy', ring('gy', -1))  6.24 us
    ppermute x2, starting transfers between devices, shards(): from_right = lax.ppermute(left_msg, 'gx', ring('gx', -1))  5.91 us
  transfers between devices with their start and end apart: 9, of which 6 were waited for; matrix products, arithmetic and copies ran while one was open for 2% of the time, Pallas kernels for 8%

commit v1 on v0

v1 whole, which is shorter than its diff:
```python
import jax
import jax.numpy as jnp
from jax import lax
from jax.experimental import pallas as pl
from jax.experimental.pallas import tpu as pltpu
from jax.sharding import PartitionSpec as P

VELOCITIES = [
    (0, 0, 0),
    (1, 0, 0),
    (-1, 0, 0),
    (0, 1, 0),
    (0, -1, 0),
    (0, 0, 1),
    (0, 0, -1),
    (1, 1, 0),
    (-1, -1, 0),
    (1, -1, 0),
    (-1, 1, 0),
    (1, 0, 1),
    (-1, 0, -1),
    (1, 0, -1),
    (-1, 0, 1),
    (0, 1, 1),
    (0, -1, -1),
    (0, 1, -1),
    (0, -1, 1),
]
WEIGHTS = [1.0 / 3.0] + [1.0 / 18.0] * 6 + [1.0 / 36.0] * 12
OPPOSITE = [0] + [q + 1 if q % 2 else q - 1 for q in range(1, 19)]
OMEGA = 1.6
F32 = jnp.float32
BF16 = jnp.bfloat16
EXACT = lax.Precision.HIGHEST

POP_TILES = 152
SEED_TILES = 76
LIST_TILES = 8
X_TILES = POP_TILES + SEED_TILES
Y_TILES = 38 + 19 + LIST_TILES
SIDE_COUNT = (3, 2, 1, 1)
SIDE_BASE = (0, 3, 5, 6)


def full(shape=None):
    return pl.BlockSpec(memory_space=pltpu.VMEM)


def row_iota(shape):
    return lax.broadcasted_iota(jnp.int32, shape, 0)


def signs(dirs, component):
    out = jnp.zeros(dirs.shape, F32)
    for q in range(1, 19):
        c = VELOCITIES[q][component]
        if c:
            out = jnp.where(dirs == q, float(c), out)
    return out


def low_half(shape):
    return lax.broadcasted_iota(jnp.int32, shape, len(shape) - 2) < 4


def front_kernel(
    base,
    live_hbm,
    pops_hbm,
    seed_hbm,
    wall_hbm,
    cell_hbm,
    dirs_hbm,
    node_hbm,
    table_hbm,
    up_msg,
    down_msg,
    lists,
    wall_copies,
    pops,
    seed,
    wall,
    cell,
    dirs,
    node,
    table,
    live,
    sems,
):
    pairs = (
        (wall_hbm, wall),
        (node_hbm, node),
        (table_hbm, table),
        (dirs_hbm, dirs),
        (cell_hbm, cell),
        (pops_hbm, pops),
        (seed_hbm, seed),
        (live_hbm, live),
    )
    copies = [pltpu.make_async_copy(a, b, sems.at[i]) for i, (a, b) in enumerate(pairs)]
    for copy in copies:
        copy.start()
    copies[0].wait()
    row = jnp.concatenate([wall[c : c + 1, :] for c in range(3)], axis=1)
    wall_copies[...] = jnp.broadcast_to(row.reshape(1, 1, 192), (32, 1, 192))
    for copy in copies[1:5] + copies[7:]:
        copy.wait()
    front_links(base, live, cell, dirs, node, table, up_msg, down_msg, lists)
    copies[5].wait()
    copies[6].wait()
    low = low_half((8, 128))
    pair = row_iota((8, 128)) // 2
    for q in range(19):
        for i in range(2):
            even = pops[q, 2 * i]
            odd = pltpu.roll(pops[q, 2 * i + 1], 4, 0)
            down_msg[2 * q + i] = jnp.where(low, even, odd)
            up_msg[2 * q + i] = jnp.where(low, odd, even)
        down_msg[38 + q], up_msg[38 + q] = edge_rows([seed[q, x] for x in range(4)], pair)


def front_links(base, live, cell, dirs, node, table, up_msg, down_msg, lists):
    slot_table = table[...]
    high = (slot_table // 128).astype(F32).astype(BF16)
    rest = (slot_table % 128).astype(F32).astype(BF16)
    both = jnp.concatenate([high, rest], axis=0)
    iota = iota256()
    lanes = row_iota((128, 1024))
    lane = lax.broadcasted_iota(jnp.int32, (1, 1024), 1)
    codes, owners = [], []
    for s in range(4):
        nodes = node[s : s + 1, :]
        hot = onehot((nodes % 128).astype(F32), 128, iota)
        picked = jnp.dot(both, hot, preferred_element_type=F32)
        match = lanes == nodes // 128
        slot_high = jnp.sum(jnp.where(match, picked[:128], 0.0), axis=0, keepdims=True)
        slot_rest = jnp.sum(jnp.where(match, picked[128:], 0.0), axis=0, keepdims=True)
        owners.append(slot_high * 128.0 + slot_rest - base[0].astype(F32))
        direction = dirs[s : s + 1, :]
        opposite = direction + 1 - 2 * ((direction + 1) % 2)
        code = opposite * 4096 + cell[s : s + 1, :]
        codes.append(jnp.where(lane < live[s], code, -1).astype(F32))
    table8 = jnp.concatenate(codes + owners, axis=0)
    lists[...] = table8
    for t in range(8):
        up_msg[57 + t] = table8[:, 128 * t : 128 * t + 128]
        down_msg[57 + t] = table8[:, 128 * t : 128 * t + 128]


def edge_rows(columns, pair):
    down = columns[0]
    up = pltpu.roll(columns[0], 2, 0)
    for x in range(1, 4):
        down = jnp.where(pair == x, pltpu.roll(columns[x], 2 * x, 0), down)
        up = jnp.where(pair == x, pltpu.roll(columns[x], 2 * x + 2, 0) if x < 3 else columns[x], up)
    return down, up


def push_kernel(wall, lists, from_up, from_down, out):
    owned = wall[...].reshape(32, 192)
    speeds = jnp.concatenate([owned[:, 64 * c : 64 * c + 64] for c in range(3)], axis=0)
    high = speeds.astype(BF16)
    rest = (speeds - high.astype(F32)).astype(BF16)
    last = (speeds - high.astype(F32) - rest.astype(F32)).astype(BF16)
    pieces = jnp.concatenate([high, rest, last], axis=0)
    iota = iota256()
    owner_iota = row_iota((32, 1024)).astype(F32)
    for k, table8 in enumerate((lists[...], read_list(from_up, 57), read_list(from_down, 57))):
        out[8 * k : 8 * k + 4, :] = table8[:4]
        for s in range(4):
            slot = table8[4 + s : 5 + s, :]
            owner = jnp.floor(slot * (1.0 / 64.0))
            place = slot - owner * 64.0
            picked = jnp.dot(pieces, onehot(place, 64, iota), preferred_element_type=F32)
            picked = picked[:96] + picked[96:192] + picked[192:]
            match = owner_iota == owner
            opposite = table8[s : s + 1, :].astype(jnp.int32) // 4096
            push = jnp.zeros((1, 1024), F32)
            for c in range(3):
                speed = jnp.sum(
                    jnp.where(match, picked[32 * c : 32 * c + 32], 0.0), axis=0, keepdims=True
                )
                push = push - signs(opposite, c) * speed
            out[8 * k + 4 + s : 8 * k + 5 + s, :] = push


def pack_kernel(pops, seed, from_up, from_down, right_msg, left_msg):
    low = low_half((8, 128))
    sub = row_iota((8, 128))
    for q in range(19):
        for i in range(2):
            up = from_up[2 * q + i]
            down = from_down[2 * q + i]
            even = jnp.where(low, up, down)
            odd = pltpu.roll(jnp.where(low, down, up), 4, 0)
            for x, halo in ((2 * i, even), (2 * i + 1, odd)):
                k = (q * 4 + x) * 2
                own = pops[q, x]
                for msg in (right_msg, left_msg):
                    msg[k] = own
                    msg[k + 1] = halo
        up = from_up[38 + q]
        down = from_down[38 + q]
        for x in range(4):
            halo = widen_two(up, down, x, sub)
            msg = left_msg if x < 2 else right_msg
            k = POP_TILES + (q * 2 + x % 2) * 2
            msg[k] = seed[q, x]
            msg[k + 1] = halo


def widen_two(up, down, x, sub):
    first = up if x == 0 else pltpu.roll(up, 8 - 2 * x, 0)
    last = down if x == 3 else pltpu.roll(down, 6 - 2 * x, 0)
    return jnp.where(sub < 4, first, last)


def onehot(code, rows, iota):
    out = []
    padded = (rows + 15) // 16 * 16
    for start in range(0, padded, 256):
        count = min(256, padded - start)
        wanted = jnp.clip(code - float(start), -1.0, 256.0).astype(BF16)
        out.append(
            jnp.concatenate(
                [
                    jnp.where(
                        iota[:count] == wanted[:, 128 * t : 128 * t + 128],
                        jnp.array(1.0, BF16),
                        jnp.array(0.0, BF16),
                    )
                    for t in range(8)
                ],
                axis=1,
            )
        )
    return out[0] if len(out) == 1 else jnp.concatenate(out, axis=0)


def iota256():
    return row_iota((256, 128)).astype(F32).astype(BF16)


def split_code(code):
    number = code.astype(jnp.int32)
    dead = number < 0
    z = jnp.where(dead, -1, number % 128)
    row = jnp.where(dead, 0, number // 128)
    return dead, row // 32 - 1, (row // 8) % 4, row % 8, z


def scatter_table(code, push, first, count, iota, part):
    dead, lane_q, x, y, z = split_code(code)
    index = lane_q * count + (x - first)
    outside = dead | (x < first) | (x >= first + count)
    if part == "all":
        row, rows = index * 8 + y, 144 * count
    elif part == "low":
        row, rows = index * 4 + y, 72 * count
        outside = outside | (y >= 4)
    else:
        row, rows = (index + 1 - 2 * (index % 2)) * 4 + y - 4, 72 * count
        outside = outside | (y < 4)
    target = onehot(jnp.where(outside, -1, row).astype(F32), rows, iota)
    zcode = z.astype(F32).astype(BF16)
    high = push.astype(BF16)
    mid = (push - high.astype(F32)).astype(BF16)
    last = (push - high.astype(F32) - mid.astype(F32)).astype(BF16)
    zero = jnp.array(0.0, BF16)
    blocks = [[], [], [], []]
    for t in range(8):
        cut = slice(128 * t, 128 * t + 128)
        match = iota[:128] == zcode[:, cut]
        blocks[0].append(jnp.where(match, jnp.array(1.0, BF16), zero))
        for b, piece in zip(blocks[1:], (high, mid, last)):
            b.append(jnp.where(match, piece[:, cut], zero))
    values = jnp.concatenate([jnp.concatenate(b, axis=1) for b in blocks], axis=0)
    dense = lax.dot_general(
        target, values, (((1,), (1,)), ((), ())), preferred_element_type=F32
    )[:rows]
    return dense[:, :128], dense[:, 128:256] + dense[:, 256:384] + dense[:, 384:]


def scatter_columns(lists, s, index, first, count, iota, n_ref, s_ref, where):
    own, up, down = lists
    n, p = scatter_table(own[s : s + 1, :], own[4 + s : 5 + s, :], first, count, iota, "all")
    at = pl.ds(where, count)
    n_ref[index, :, at, 0:8, :] = n.reshape(18, count, 8, 128)
    s_ref[index, :, at, 0:8, :] = p.reshape(18, count, 8, 128)
    above = scatter_table(up[s : s + 1, :], up[4 + s : 5 + s, :], first, count, iota, "low")
    below = scatter_table(down[s : s + 1, :], down[4 + s : 5 + s, :], first, count, iota, "high")
    shape = (9 * count, 8, 128)
    low = low_half(shape)
    for ref, a, b in zip((n_ref, s_ref), above, below):
        a, b = a.reshape(shape), b.reshape(shape)
        even = jnp.where(low, a, b)
        odd = pltpu.roll(jnp.where(low, b, a), 4, 1)
        halo = jnp.stack([even, odd], axis=1).reshape(18, count, 8, 128)
        ref[index, :, at, 8:16, :] = halo


def read_list(ref, start):
    return jnp.concatenate([ref[start + t] for t in range(8)], axis=1)


def own_links_kernel(lists, n_ref, s_ref):
    iota = iota256()
    three = [lists[8 * k : 8 * k + 8, :] for k in range(3)]
    for s in range(4):
        scatter_columns(three, s, s, 0, 4, iota, n_ref, s_ref, 0)


def side_links_kernel(from_left, from_right, n_ref, s_ref):
    iota = iota256()
    for side, ref in enumerate((from_left, from_right)):
        three = [ref[8 * k : 8 * k + 8, :] for k in range(3)]
        for s in range(4):
            count = SIDE_COUNT[s]
            first = 0 if side else 4 - count
            scatter_columns(three, s, side, first, count, iota, n_ref, s_ref, SIDE_BASE[s])


def column_groups(s, n_own, s_own, n_side, s_side):
    count, base = SIDE_COUNT[s], SIDE_BASE[s]
    return (
        (4 - count, count, lambda q, i: n_side[0, q, base + i], lambda q, i: s_side[0, q, base + i]),
        (4, 4, lambda q, i: n_own[s, q, i], lambda q, i: s_own[s, q, i]),
        (8, count, lambda q, i: n_side[1, q, base + i], lambda q, i: s_side[1, q, base + i]),
    )


def shifted(value, cy, cz):
    if cy:
        value = pltpu.roll(value, cy % 16, 0)
    if cz:
        value = pltpu.roll(value, cz % 128, 1)
    return value


def moments(f):
    rho = f[0]
    for q in range(1, 19):
        rho = rho + f[q]
    inverse = 1.0 / rho
    speeds = []
    for c in range(3):
        total = None
        for q in range(1, 19):
            v = VELOCITIES[q][c]
            if v:
                total = (f[q] if v > 0 else -f[q]) if total is None else (total + f[q] if v > 0 else total - f[q])
        speeds.append(total * inverse)
    return rho, speeds


def along(speeds, q):
    total = None
    for c in range(3):
        v = VELOCITIES[q][c]
        if v:
            term = speeds[c] if v > 0 else -speeds[c]
            total = term if total is None else total + term
    return total


def collide_column(f):
    rho, speeds = moments(f)
    rest = 1.0 - 1.5 * (speeds[0] * speeds[0] + speeds[1] * speeds[1] + speeds[2] * speeds[2])
    out = [(1.0 - OMEGA) * f[0] + (OMEGA * WEIGHTS[0]) * rho * rest]
    for q in range(1, 19, 2):
        cu = along(speeds, q)
        scale = (OMEGA * WEIGHTS[q]) * rho
        even = scale * (rest + 4.5 * cu * cu)
        odd = scale * (3.0 * cu)
        out.append((1.0 - OMEGA) * f[q] + (even + odd))
        out.append((1.0 - OMEGA) * f[q + 1] + (even - odd))
    return out, rho


def collide_into(load, start, count, relaxed, density):
    def body(i, carry):
        f = [load(q, i) for q in range(19)]
        g, rho = collide_column(f)
        for q in range(19):
            relaxed[q, start + i] = g[q]
        density[start + i] = rho
        return carry

    lax.fori_loop(0, count, body, 0)


def stream_into(relaxed, density, groups, out):
    for start, count, counts, pushes in groups:

        def body(i, carry):
            x = start + i
            rho = density[x]
            out[0, x] = relaxed[0, x]
            for q in range(1, 19):
                p = OPPOSITE[q]
                cx, cy, cz = VELOCITIES[q]
                moved = shifted(relaxed[q, x - cx], cy, cz)
                bounce = (0.5 * counts(q - 1, i)) * (relaxed[p, x] - relaxed[q, x])
                push = (6.0 * WEIGHTS[q]) * rho * pushes(q - 1, i)
                out[q, x] = moved + (bounce - push)
            return carry

        lax.fori_loop(0, count, body, 0)


def adjoint_column(f, arrived, local, counts, pushes):
    rho, speeds = moments(f)
    b = [arrived[0]]
    direct = None
    for q in range(1, 19):
        p = OPPOSITE[q]
        b.append(
            arrived[q] + 0.5 * (counts[p - 1] * local[p] - counts[q - 1] * local[q])
        )
        term = (6.0 * WEIGHTS[q]) * (pushes[q - 1] * local[q])
        direct = term if direct is None else direct + term
    beta = [WEIGHTS[q] * b[q] for q in range(19)]
    total = beta[0]
    first = [None] * 3
    second = [None] * 3
    for q in range(1, 19, 2):
        plus = beta[q] + beta[q + 1]
        minus = beta[q] - beta[q + 1]
        total = total + plus
        inner = along(speeds, q) * plus
        for c in range(3):
            v = VELOCITIES[q][c]
            if v:
                m = minus if v > 0 else -minus
                k = inner if v > 0 else -inner
                first[c] = m if first[c] is None else first[c] + m
                second[c] = k if second[c] is None else second[c] + k
    square = speeds[0] * speeds[0] + speeds[1] * speeds[1] + speeds[2] * speeds[2]
    curved = speeds[0] * second[0] + speeds[1] * second[1] + speeds[2] * second[2]
    rest = OMEGA * (total - 4.5 * curved + 1.5 * square * total) - direct
    slopes = [
        OMEGA * (3.0 * first[c] + 9.0 * second[c] - 3.0 * speeds[c] * total) for c in range(3)
    ]
    out = [(1.0 - OMEGA) * b[0] + rest]
    for q in range(1, 19, 2):
        cu = along(slopes, q)
        out.append((1.0 - OMEGA) * b[q] + (rest + cu))
        out.append((1.0 - OMEGA) * b[q + 1] + (rest - cu))
    return out, rho


def adjoint_at(load_f, adjoint, x, counts, pushes):
    f = [load_f(q) for q in range(19)]
    local = [adjoint(q, x) for q in range(19)]
    arrived = []
    for q in range(19):
        cx, cy, cz = VELOCITIES[q]
        value = adjoint(q, x + cx) if cx else local[q]
        arrived.append(shifted(value, -cy, -cz))
    out, rho = adjoint_column(
        f, arrived, local, [counts(q) for q in range(18)], [pushes(q) for q in range(18)]
    )
    return out, rho, local


def ext(ref, k):
    return jnp.concatenate([ref[k], ref[k + 1]], axis=0)


def window_kernel(
    right_msg,
    left_msg,
    from_left,
    from_right,
    n_own,
    s_own,
    n_side,
    s_side,
    f1_out,
    a2_out,
    up_msg,
    down_msg,
    pull,
    relaxed,
    density,
    f2,
    f3,
    a4,
    a3,
):
    def groups(s):
        return column_groups(s, n_own, s_own, n_side, s_side)

    for ref, start in ((from_left, 0), (right_msg, 4), (from_right, 8)):

        def load(q, i, ref=ref):
            return ref[pl.ds((q * 4 + i) * 2, 2)].reshape(16, 128)

        collide_into(load, start, 4, relaxed, density)
    stream_into(relaxed, density, groups(0), f2)
    for q in range(19):
        f1_out[q] = f2[q, 3:9]
    collide_into(lambda q, i: f2[q, 1 + i], 1, 10, relaxed, density)
    stream_into(relaxed, density, groups(1), f2)
    collide_into(lambda q, i: f2[q, 2 + i], 2, 8, relaxed, density)
    stream_into(relaxed, density, groups(2), f3)
    for q in range(19):
        for x in range(2):
            k = POP_TILES + (q * 2 + x) * 2
            a4[q, 2 + x] = ext(from_left, k)
            a4[q, 4 + x] = ext(left_msg, k)
            a4[q, 6 + x] = ext(right_msg, k)
            a4[q, 8 + x] = ext(from_right, k)
    for start, count, counts, pushes in groups(3):

        def third(i, carry, start=start, count=count, counts=counts, pushes=pushes):
            x = start + i
            out, rho, local = adjoint_at(
                lambda q: f3[q, x],
                lambda q, at: a4[q, at],
                x,
                lambda q: counts(q, i),
                lambda q: pushes(q, i),
            )
            for q in range(19):
                a3[q, x] = out[q]
            if count == 4:
                for q in range(1, 19):
                    pull[0, q - 1, i] = ((-6.0 * WEIGHTS[q]) * rho * local[q])[:8]
            return carry

        lax.fori_loop(0, count, third, 0)

    def second(i, carry):
        x = 4 + i
        out, rho, local = adjoint_at(
            lambda q: f2[q, x],
            lambda q, at: a3[q, at],
            x,
            lambda q: n_own[2, q, i],
            lambda q: s_own[2, q, i],
        )
        rho1 = f1_out[0, 1 + i]
        for q in range(1, 19):
            rho1 = rho1 + f1_out[q, 1 + i]
        for q in range(19):
            a2_out[q, i] = out[q][:8]
        for q in range(1, 19):
            pull[1, q - 1, i] = ((-6.0 * WEIGHTS[q]) * rho * local[q])[:8]
            pull[2, q - 1, i] = ((-6.0 * WEIGHTS[q]) * rho1 * out[q])[:8]
        return carry

    lax.fori_loop(0, 4, second, 0)
    pair = row_iota((8, 128)) // 2
    for q in range(19):
        down_msg[q], up_msg[q] = edge_rows([a2_out[q, x] for x in range(4)], pair)


OUTWARD = tuple(tuple(q for q in range(19) if VELOCITIES[q][0] == c) for c in (-1, 1))
A_TILES = 48


def pack_adjoint_kernel(a2, from_up, from_down, right_msg, left_msg, middle):
    sub = row_iota((8, 128))
    for q in range(19):
        for x in range(4):
            own, halo = a2[q, x], widen_two(from_up[q], from_down[q], x, sub)
            if x in (0, 3):
                msg, k = (left_msg if x == 0 else right_msg), 2 * q
            else:
                msg, k = middle, (q * 2 + x - 1) * 2
            msg[k] = own
            msg[k + 1] = halo
            for side, edge in ((right_msg, 0), (left_msg, 1)):
                if x == 2 - edge and q in OUTWARD[edge]:
                    k = 38 + 2 * OUTWARD[edge].index(q)
                    side[k] = own
                    side[k + 1] = halo


def link_gradient(pulls, lists, steps):
    iota = iota256()
    total = jnp.zeros((32, 192), F32)
    lanes = row_iota((128, 1024))
    for i, s in enumerate(steps):
        code = lists[s : s + 1, :]
        dead, lane_q, x, y, z = split_code(code)
        row = jnp.where(dead, -1, lane_q * 32 + x * 8 + y).astype(F32)
        hot = onehot(row, 576, iota)
        high = pulls[i].astype(BF16)
        rest = (pulls[i] - high.astype(F32)).astype(BF16)
        low = (pulls[i] - high.astype(F32) - rest.astype(F32)).astype(BF16)
        picked = lax.dot_general(
            jnp.concatenate([high, rest, low], axis=1),
            hot,
            (((0,), (0,)), ((), ())),
            preferred_element_type=F32,
        )
        match = lanes == z
        value = jnp.sum(
            jnp.where(match, picked[:128] + picked[128:256] + picked[256:], 0.0),
            axis=0,
            keepdims=True,
        )
        slot = lists[4 + s : 5 + s, :].astype(jnp.int32)
        opposite = code.astype(jnp.int32) // 4096
        owner = jnp.where(row_iota((32, 1024)) == slot // 64, 1.0, 0.0)
        place = row_iota((64, 1024)) == slot % 64
        parts = jnp.concatenate(
            [jnp.where(place, -value * signs(opposite, c), 0.0) for c in range(3)], axis=0
        )
        total = total + lax.dot_general(
            owner,
            parts,
            (((1,), (1,)), ((), ())),
            precision=EXACT,
            preferred_element_type=F32,
        )
    return total


def late_links_kernel(pull, lists, out):
    pulls = [pull[i].reshape(576, 128) for i in range(2)]
    out[...] = link_gradient(pulls, lists, (3, 2))


def early_links_kernel(pull, lists, late, out):
    out[...] = late[...] + link_gradient([pull[2].reshape(576, 128)], lists, (1,))


def first_adjoint_kernel(
    right_msg,
    left_msg,
    middle,
    from_left,
    from_right,
    pops,
    f1,
    n_own,
    s_own,
    n_side,
    s_side,
    late,
    lists,
    a1,
    grad_out,
    a2,
    pull,
):
    for q in range(19):
        a2[q, 1] = ext(from_left, 2 * q)
        a2[q, 2] = ext(left_msg, 2 * q)
        a2[q, 3] = ext(middle, 4 * q)
        a2[q, 4] = ext(middle, 4 * q + 2)
        a2[q, 5] = ext(right_msg, 2 * q)
        a2[q, 6] = ext(from_right, 2 * q)
    for i in range(5):
        a2[OUTWARD[0][i], 0] = ext(from_left, 38 + 2 * i)
        a2[OUTWARD[1][i], 7] = ext(from_right, 38 + 2 * i)
    left, own, right = column_groups(1, n_own, s_own, n_side, s_side)
    for at, count, group, skip in ((0, 1, left, 1), (1, 4, own, 0), (5, 1, right, 0)):

        def first(i, carry, at=at, count=count, group=group, skip=skip):
            out, rho, local = adjoint_at(
                lambda q: f1[q, at + i],
                lambda q, x: a2[q, x],
                at + i + 1,
                lambda q: group[2](q, i + skip),
                lambda q: group[3](q, i + skip),
            )
            for q in range(19):
                a1[q, at + i] = out[q]
            if count == 4:
                rho0 = pops[0, i]
                for q in range(1, 19):
                    rho0 = rho0 + pops[q, i]
                for q in range(1, 19):
                    pull[q - 1, i] = (-6.0 * WEIGHTS[q]) * rho0 * out[q][:8]
            return carry

        lax.fori_loop(0, count, first, 0)
    total = late[...] + link_gradient([pull[...].reshape(576, 128)], lists, (0,))
    grad_out[...] = total.reshape(32, 1, 192)


def total_kernel(parts, out):
    total = parts[0]
    for k in range(1, 32):
        total = total + parts[k]
    for c in range(3):
        out[c : c + 1, :] = total[:, 64 * c : 64 * c + 64]


def last_adjoint_kernel(a1, pops, n_own, s_own, a0_out):
    def last(i, carry):
        f = [pops[q, i] for q in range(19)]
        local = [a1[q, 1 + i] for q in range(19)]
        arrived = []
        for q in range(19):
            cx, cy, cz = VELOCITIES[q]
            value = a1[q, 1 + i + cx] if cx else local[q]
            arrived.append(shifted(value, -cy, -cz)[:8])
        local = [v[:8] for v in local]
        out, _ = adjoint_column(
            f,
            arrived,
            local,
            [n_own[0, q, i, 0:8] for q in range(18)],
            [s_own[0, q, i, 0:8] for q in range(18)],
        )
        for q in range(19):
            a0_out[q, i] = out[q]
        return carry

    lax.fori_loop(0, 4, last, 0)


def ring(axis, step):
    count = lax.axis_size(axis)
    return [(i, (i + step) % count) for i in range(count)]


def shape(*dims, dtype=F32):
    return jax.ShapeDtypeStruct(dims, dtype)


def cost(flops, bytes_accessed):
    return pl.CostEstimate(flops=flops, bytes_accessed=bytes_accessed, transcendentals=0)


def call(kernel, name, out_shape, count, limit, scratch=(), smem=0, flops=0, moved=0):
    vmem = full()
    many = isinstance(out_shape, list)
    return pl.pallas_call(
        kernel,
        name=name,
        out_shape=out_shape,
        in_specs=[pl.BlockSpec(memory_space=pltpu.SMEM)] * smem + [vmem] * (count - smem),
        out_specs=[vmem] * len(out_shape) if many else vmem,
        scratch_shapes=list(scratch),
        cost_estimate=cost(flops, moved) if flops else None,
        compiler_params=pltpu.CompilerParams(vmem_limit_bytes=limit << 20),
    )


def shards(
    populations, wall_speed, adjoint_seed, link_cell, link_dir, link_node, live_links, node_slot
):
    base = (lax.axis_index("gx") * 2048).astype(jnp.int32).reshape(1)
    smem = pl.BlockSpec(memory_space=pltpu.SMEM)
    operands = (
        populations,
        adjoint_seed,
        wall_speed,
        link_cell,
        link_dir,
        link_node,
        node_slot.reshape(128, 128),
    )
    up_msg, down_msg, lists, copies = pl.pallas_call(
        front_kernel,
        name="front",
        out_shape=[
            shape(Y_TILES, 8, 128),
            shape(Y_TILES, 8, 128),
            shape(8, 1024),
            shape(32, 1, 192),
        ],
        in_specs=[smem] + [pl.BlockSpec(memory_space=pltpu.HBM)] * 8,
        out_specs=[full()] * 4,
        scratch_shapes=[pltpu.VMEM(a.shape, a.dtype) for a in operands]
        + [pltpu.SMEM((4,), jnp.int32), pltpu.SemaphoreType.DMA((8,))],
        compiler_params=pltpu.CompilerParams(vmem_limit_bytes=12 << 20),
    )(
        base,
        *(
            pltpu.with_memory_space_constraint(a, pltpu.HBM)
            for a in (live_links.reshape(4), *operands)
        ),
    )
    from_down = lax.ppermute(up_msg, "gy", ring("gy", 1))
    from_up = lax.ppermute(down_msg, "gy", ring("gy", -1))
    wall = lax.all_to_all(copies, "gy", split_axis=0, concat_axis=0, tiled=True)
    all_lists = call(push_kernel, "push", shape(24, 1024), 4, 8, flops=500_000_000, moved=500_000)(
        wall, lists, from_up, from_down
    )
    left_lists = lax.ppermute(all_lists, "gx", ring("gx", 1))
    right_lists = lax.ppermute(all_lists, "gx", ring("gx", -1))
    right_msg, left_msg = call(pack_kernel, "pack", [shape(X_TILES, 8, 128)] * 2, 4, 8)(
        populations, adjoint_seed, from_up, from_down
    )
    from_left = lax.ppermute(right_msg, "gx", ring("gx", 1))
    from_right = lax.ppermute(left_msg, "gx", ring("gx", -1))
    n_own, s_own = call(
        own_links_kernel,
        "own_links",
        [shape(4, 18, 4, 16, 128)] * 2,
        1,
        24,
        flops=5_000_000_000,
        moved=5_000_000,
    )(all_lists)
    n_side, s_side = call(
        side_links_kernel,
        "side_links",
        [shape(2, 18, 7, 16, 128)] * 2,
        2,
        24,
        flops=5_000_000_000,
        moved=5_000_000,
    )(left_lists, right_lists)
    region = pltpu.VMEM((19, 12, 16, 128), F32)
    f1, a2, up_msg, down_msg, pull = call(
        window_kernel,
        "window",
        [
            shape(19, 6, 16, 128),
            shape(19, 4, 8, 128),
            shape(19, 8, 128),
            shape(19, 8, 128),
            shape(3, 18, 4, 8, 128),
        ],
        8,
        30,
        [region, pltpu.VMEM((12, 16, 128), F32), region, region, region, region],
    )(right_msg, left_msg, from_left, from_right, n_own, s_own, n_side, s_side)
    from_down = lax.ppermute(up_msg, "gy", ring("gy", 1))
    from_up = lax.ppermute(down_msg, "gy", ring("gy", -1))
    late = call(
        late_links_kernel, "late_links", shape(32, 192), 2, 16, flops=2_000_000_000, moved=2_000_000
    )(pull, lists)
    late, from_up, from_down = lax.optimization_barrier((late, from_up, from_down))
    right_msg, left_msg, middle = call(
        pack_adjoint_kernel,
        "pack_adjoint",
        [shape(A_TILES, 8, 128), shape(A_TILES, 8, 128), shape(SEED_TILES, 8, 128)],
        3,
        4,
    )(a2, from_up, from_down)
    from_left = lax.ppermute(right_msg, "gx", ring("gx", 1))
    from_right = lax.ppermute(left_msg, "gx", ring("gx", -1))
    late = call(
        early_links_kernel,
        "early_links",
        shape(32, 192),
        3,
        16,
        flops=1_000_000_000,
        moved=1_000_000,
    )(pull, lists, late)
    a1, owned = call(
        first_adjoint_kernel,
        "first_adjoint",
        [shape(19, 6, 16, 128), shape(32, 1, 192)],
        13,
        24,
        [pltpu.VMEM((19, 8, 16, 128), F32), pltpu.VMEM((18, 4, 8, 128), F32)],
    )(
        right_msg,
        left_msg,
        middle,
        from_left,
        from_right,
        populations,
        f1,
        n_own,
        s_own,
        n_side,
        s_side,
        late,
        lists,
    )
    arrived = lax.all_to_all(owned, "gy", split_axis=0, concat_axis=0, tiled=True)
    adjoint = call(
        last_adjoint_kernel,
        "last_adjoint",
        shape(19, 4, 8, 128),
        4,
        12,
        flops=10_000_000,
        moved=4_000_000,
    )(a1, populations, n_own, s_own)
    gradient = call(total_kernel, "total", shape(3, 64), 1, 4)(arrived)
    return (adjoint, gradient)


def solution(mesh):
    placed = (
        P(None, "gx", "gy", None),
        P(None, ("gx", "gy")),
        P(None, "gx", "gy", None),
        P(None, ("gx", "gy")),
        P(None, ("gx", "gy")),
        P(None, ("gx", "gy")),
        P(None, ("gx", "gy")),
        P(),
    )
    return jax.shard_map(
        shards,
        mesh=mesh,
        in_specs=placed,
        out_specs=(P(None, "gx", "gy", None), P(None, ("gx", "gy"))),
        check_vma=False,
    )
```

time: 118 us -> 86.9 us (0.74)
  waiting for transfers between devices: 19.9 us -> 6.18 us
  local copies, waits for them, and re-layouts: 13.6 us -> 3.79 us
  Pallas kernels: 42.5 us -> 34.5 us
  blocking collectives: 16.5 us -> 21.9 us
  starting transfers between devices: 24.4 us -> 19.1 us
    pallas_call x7 -> x12, Pallas kernels: 42.5 us -> 34.5 us  [the longest x1 8.26 us: shards(): call(side_links_kernel, 'side_links', [shape(2, 18, 7, 16, 128)] * 2, 2,...]
    ppermute x2, waiting for transfers between devices: 7.22 us -> 0.05 us  [shards(): from_up = lax.ppermute(down_msg, 'gy', ring('gy', -1))]
    unnamed x44 -> x12, local copies, waits for them, and re-layouts: 10.1 us -> 3.79 us
    all_to_all x1, blocking collectives: 16.5 us -> 21.9 us  [shards(): wall = lax.all_to_all(copies, 'gy', split_axis=0, concat_axis=0, tiled=True)]
    ppermute x2, waiting for transfers between devices: 3.44 us -> 0.01 us  [shards(): from_down = lax.ppermute(up_msg, 'gy', ring('gy', 1))]
    all_to_all x1, starting transfers between devices: 11.7 us -> 8.32 us  [shards(): lax.all_to_all(owned, 'gy', split_axis=0, concat_axis=0, tiled=True)]
    all_to_all x1, waiting for transfers between devices: 7.32 us -> 4.63 us  [shards(): lax.all_to_all(owned, 'gy', split_axis=0, concat_axis=0, tiled=True)]
    ppermute x2, starting transfers between devices: 6.24 us -> 3.78 us  [shards(): from_up = lax.ppermute(down_msg, 'gy', ring('gy', -1))]
  transfers between devices with their start and end apart: 9 -> 11, of which waited for: 6 -> 2; matrix products, arithmetic and copies ran while one was open for 2% -> 0% of each run, Pallas kernels for 8% -> 24%
where the time goes in v1:
time: 86.9 us; the launch traced here: 86.3 us
  Pallas kernels  34.5 us (40%)
  blocking collectives  21.9 us (25%)
  starting transfers between devices  19.1 us (22%)
  waiting for transfers between devices  6.18 us (7%)
  local copies, waits for them, and re-layouts  3.79 us (4%)
    all_to_all x1, blocking collectives, shards(): wall = lax.all_to_all(copies, 'gy', split_axis=0, concat_axis=0, tiled=True)  21.9 us
    all_to_all x1, starting transfers between devices, shards(): lax.all_to_all(owned, 'gy', split_axis=0, concat_axis=0, tiled=True)  8.32 us
    pallas_call x1, Pallas kernels, shards(): call(side_links_kernel, 'side_links', [shape(2, 18, 7, 16, 128)] * 2, 2,...  8.26 us
    pallas_call x1, Pallas kernels, shards(): call(window_kernel, 'window', [shape(19, 6, 16, 128), shape(19, 4, 8, 128...  5.73 us
    pallas_call x1, Pallas kernels, shards(): call(own_links_kernel, 'own_links', [shape(4, 18, 4, 16, 128)] * 2, 1, 24...  5.1 us
    ppermute x2, starting transfers between devices, shards(): from_right = lax.ppermute(left_msg, 'gx', ring('gx', -1))  4.78 us
    all_to_all x1, waiting for transfers between devices, shards(): lax.all_to_all(owned, 'gy', split_axis=0, concat_axis=0, tiled=True)  4.63 us
    pallas_call x1, Pallas kernels, shards(): call(late_links_kernel, 'late_links', shape(32, 192), 2, 16, flops=200000...  4.26 us
  transfers between devices with their start and end apart: 11, of which 2 were waited for; matrix products, arithmetic and copies ran while one was open for 0% of the time, Pallas kernels for 24%

profile of v1, /device:TPU:8, one launch (start us, length us, event | category | flops | bytes accessed | tf_op | source)
XLA Modules:
  0.0 86.3 jit_solution(11048453254810384998)
XLA Ops:
  0.7 2.0 %front.1 = (f32[65,8,128]{2,1,0:T(8,128)S(1)}, f32[65,8,128]{2,1,0:T(8,128)S(1)}, f32[8,1024]{1,0:T(8,128)S(1)}, f32[32,1,192]{2,1,0:T(1,128)S(1)}) custom-call(s32[1]{0:T(128)} %bitcast.base, s32[4]{0:T(128)} %bitcast.4, f32[19,4,8,128]{3,2,1,0:T(8,128)} %pops.5, f32[19,4,8,128]{3,2,1,0:T(8,128)} %seed.1, f32[3,64]{1,0:T(4,128)} %wall_hbm.1, ...), custom_call_target="tpu_custom_call" | custom-call | tf_op jit(solution)/shard_map/front/pallas_call | solution.py:760
  2.7 2.3 %collective-permute-start = (f32[65,8,128]{2,1,0:T(8,128)S(1)}, f32[65,8,128]{2,1,0:T(8,128)S(1)}, u32[]{:S(2)}, u32[]{:S(2)}) collective-permute-start(f32[65,8,128]{2,1,0:T(8,128)S(1)} %get-tuple-element.25), channel_id=1, source_target_pairs={{0,31},{1,0},{2,1},{3,2},{4,3},{5,4},{6,5},{7,6},{8,7},{9,8},{10,9... | collective-permute-start | bytes 798728 | tf_op jit(solution)/shard_map/ppermute | solution.py:782
  4.9 21.9 %all_to_all.10.wall = f32[32,1,192]{2,1,0:T(1,128)S(1)} all-to-all(f32[32,1,192]{2,1,0:T(1,128)S(1)} %get-tuple-element.29), channel_id=1, replica_groups=mesh['gx'=8,'gy'=32] {'gy'}, dimensions={0} | all-to-all | bytes 49152 | tf_op jit(solution)/shard_map/all_to_all | solution.py:783
  26.8 2.1 %push.1.lists = f32[24,1024]{1,0:T(8,128)S(1)} custom-call(f32[32,1,192]{2,1,0:T(1,128)S(1)} %all_to_all.10.wall, f32[8,1024]{1,0:T(8,128)S(1)} %get-tuple-element.30.lists, f32[65,8,128]{2,1,0:T(8,128)S(1)} %collective-permute-done.from_up, f32[65,8,128]{2,1,0:T(8,128)S(1)} %collective-permute-done.1.from_down), custom_call_target="tpu_custom_call" | custom-call | flops 500000000 | bytes 500000 | tf_op jit(solution)/shard_map/push/pallas_call | solution.py:784
  29.1 0.3 collective-permute-start.4
  29.6 1.1 %collective-permute-start.2 = (f32[228,8,128]{2,1,0:T(8,128)S(1)}, f32[228,8,128]{2,1,0:T(8,128)S(1)}, u32[]{:S(2)}, u32[]{:S(2)}) collective-permute-start(f32[228,8,128]{2,1,0:T(8,128)S(1)} %get-tuple-element.27.right_msg), channel_id=1, source_target_pairs={{0,32},{32,64},{64,96},{96,128},{128,160},{160,192},{192,224},{224... | collective-permute-start | bytes 2801672 | tf_op jit(solution)/shard_map/ppermute | solution.py:792
  30.7 1.8 %collective-permute-start.3 = (f32[228,8,128]{2,1,0:T(8,128)S(1)}, f32[228,8,128]{2,1,0:T(8,128)S(1)}, u32[]{:S(2)}, u32[]{:S(2)}) collective-permute-start(f32[228,8,128]{2,1,0:T(8,128)S(1)} %get-tuple-element.28.left_msg), channel_id=1, source_target_pairs={{0,224},{32,0},{64,32},{96,64},{128,96},{160,128},{192,160},{224,1... | collective-permute-start | bytes 2801672 | tf_op jit(solution)/shard_map/ppermute | solution.py:793
  32.5 5.1 %own_links.1 = (f32[4,18,4,16,128]{4,3,2,1,0:T(8,128)S(1)}, f32[4,18,4,16,128]{4,3,2,1,0:T(8,128)S(1)}) custom-call(f32[24,1024]{1,0:T(8,128)S(1)} %push.1.lists), custom_call_target="tpu_custom_call" | custom-call | flops 5000000000 | bytes 5000000 | tf_op jit(solution)/shard_map/own_links/pallas_call | solution.py:794
  37.7 8.3 %side_links.1 = (f32[2,18,7,16,128]{4,3,2,1,0:T(8,128)S(1)}, f32[2,18,7,16,128]{4,3,2,1,0:T(8,128)S(1)}) custom-call(f32[24,1024]{1,0:T(8,128)S(1)} %collective-permute-done.4.from_left, f32[24,1024]{1,0:T(8,128)S(1)} %collective-permute-done.5.from_right), custom_call_target="tpu_custom_call" | custom-call | flops 5000000000 | bytes 5000000 | tf_op jit(solution)/shard_map/side_links/pallas_call | solution.py:803
  46.0 5.7 %window.1 = (f32[19,6,16,128]{3,2,1,0:T(8,128)S(1)}, f32[19,4,8,128]{3,2,1,0:T(8,128)S(1)}, f32[19,8,128]{2,1,0:T(8,128)S(1)}, f32[19,8,128]{2,1,0:T(8,128)S(1)}, f32[3,18,4,8,128]{4,3,2,1,0:T(8,128)S(1)}) custom-call(f32[228,8,128]{2,1,0:T(8,128)S(1)} %get-tuple-element.27.right_msg, f32[228,8,128]{2,1,0:T(8,128)S(1)} %get-tuple-element.28.left_msg, ...), custom_call_target="tpu_custom_call" | custom-call | tf_op jit(solution)/shard_map/window/pallas_call | solution.py:813
  51.7 1.5 %collective-permute-start.6 = (f32[19,8,128]{2,1,0:T(8,128)S(1)}, f32[19,8,128]{2,1,0:T(8,128)S(1)}, u32[]{:S(2)}, u32[]{:S(2)}) collective-permute-start(f32[19,8,128]{2,1,0:T(8,128)S(1)} %get-tuple-element.37), channel_id=1, source_target_pairs={{0,31},{1,0},{2,1},{3,2},{4,3},{5,4},{6,5},{7,6},{8,7},{9,8},{10,9... | collective-permute-start | bytes 233480 | tf_op jit(solution)/shard_map/ppermute | solution.py:828
  53.2 0.6 collective-permute-start.7
  53.8 4.3 %late_links.1.late = f32[32,192]{1,0:T(8,128)S(1)} custom-call(f32[3,18,4,8,128]{4,3,2,1,0:T(8,128)S(1)} %get-tuple-element.36.pull, f32[8,1024]{1,0:T(8,128)S(1)} %get-tuple-element.30.lists), custom_call_target="tpu_custom_call" | custom-call | flops 2000000000 | bytes 2000000 | tf_op jit(solution)/shard_map/late_links/pallas_call | solution.py:829
  58.2 2.9 %collective-permute-start.9 = (f32[48,8,128]{2,1,0:T(8,128)S(1)}, f32[48,8,128]{2,1,0:T(8,128)S(1)}, u32[]{:S(2)}, u32[]{:S(2)}) collective-permute-start(f32[48,8,128]{2,1,0:T(8,128)S(1)} %get-tuple-element.42.left_msg), channel_id=1, source_target_pairs={{0,224},{32,0},{64,32},{96,64},{128,96},{160,128},{192,160},{224,1... | collective-permute-start | bytes 589832 | tf_op jit(solution)/shard_map/ppermute | solution.py:841
  61.2 1.9 %early_links.1.late = f32[32,192]{1,0:T(8,128)S(1)} custom-call(f32[3,18,4,8,128]{4,3,2,1,0:T(8,128)S(1)} %get-tuple-element.36.pull, f32[8,1024]{1,0:T(8,128)S(1)} %get-tuple-element.30.lists, f32[32,192]{1,0:T(8,128)S(1)} %late_links.1.late), custom_call_target="tpu_custom_call" | custom-call | flops 1000000000 | bytes 1000000 | tf_op jit(solution)/shard_map/early_links/pallas_call | solution.py:842
  63.0 1.5 %collective-permute-done.8.from_left = f32[48,8,128]{2,1,0:T(8,128)S(1)} collective-permute-done((f32[48,8,128]{2,1,0:T(8,128)S(1)}, f32[48,8,128]{2,1,0:T(8,128)S(1)}, u32[]{:S(2)}, u32[]{:S(2)}) %collective-permute-start.8) | collective-permute-done | bytes 196640 | tf_op jit(solution)/shard_map/ppermute | solution.py:840
  64.5 3.2 %first_adjoint.1 = (f32[19,6,16,128]{3,2,1,0:T(8,128)S(1)}, f32[32,1,192]{2,1,0:T(1,128)}) custom-call(f32[48,8,128]{2,1,0:T(8,128)S(1)} %get-tuple-element.41.right_msg, f32[48,8,128]{2,1,0:T(8,128)S(1)} %get-tuple-element.42.left_msg, f32[76,8,128]{2,1,0:T(8,128)S(1)} %get-tuple-element.43.middle, f32[48,8,128]{2,1,0:T(8,128)S(1)} %collective-permute-done.8.from_left, ...), custom_call_target="tpu_custom_call" | custom-call | tf_op jit(solution)/shard_map/first_adjoint/pallas_call | solution.py:851
  67.7 0.9 %copy-done.4 = f32[19,6,16,128]{3,2,1,0:T(8,128)} copy-done((f32[19,6,16,128]{3,2,1,0:T(8,128)}, f32[19,6,16,128]{3,2,1,0:T(8,128)S(1)}, u32[]{:S(2)}) %copy-start.4) | copy-done | bytes 933912
  68.6 8.3 %all-to-all-start.1 = ((f32[32,1,192]{2,1,0:T(1,128)}), f32[32,1,192]{2,1,0:T(1,128)S(1)}, u32[]{:S(2)}, u32[]{:S(2)}) async-start(f32[32,1,192]{2,1,0:T(1,128)} %get-tuple-element.47), calls=%async_computation.1 | async-start | bytes 65536 | tf_op jit(solution)/shard_map/all_to_all | solution.py:873
  77.0 1.7 %copy-done.1 = f32[4,18,4,16,128]{4,3,2,1,0:T(8,128)S(1)} copy-done((f32[4,18,4,16,128]{4,3,2,1,0:T(8,128)S(1)}, f32[4,18,4,16,128]{4,3,2,1,0:T(8,128)}, u32[]{:S(2)}) %copy-start.1) | copy-done | bytes 2359320
  78.6 1.2 %copy-done.5 = f32[19,6,16,128]{3,2,1,0:T(8,128)S(1)} copy-done((f32[19,6,16,128]{3,2,1,0:T(8,128)S(1)}, f32[19,6,16,128]{3,2,1,0:T(8,128)}, u32[]{:S(2)}) %copy-start.5) | copy-done | bytes 933912
  79.8 1.2 %last_adjoint.1 = f32[19,4,8,128]{3,2,1,0:T(8,128)} custom-call(f32[19,6,16,128]{3,2,1,0:T(8,128)S(1)} %copy-done.5, f32[19,4,8,128]{3,2,1,0:T(8,128)S(1)} %copy-done.2, f32[4,18,4,16,128]{4,3,2,1,0:T(8,128)S(1)} %get-tuple-element.31.n_own, f32[4,18,4,16,128]{4,3,2,1,0:T(8,128)S(1)} %copy-done.1), custom_call_target="tpu_custom_call" | custom-call | flops 10000000 | bytes 4000000 | tf_op jit(solution)/shard_map/last_adjoint/pallas_call | solution.py:874
  81.0 4.6 %all-to-all-done.1.parts = f32[32,1,192]{2,1,0:T(1,128)S(1)} async-done(((f32[32,1,192]{2,1,0:T(1,128)}), f32[32,1,192]{2,1,0:T(1,128)S(1)}, u32[]{:S(2)}, u32[]{:S(2)}) %all-to-all-start.1) | async-done | bytes 24608 | tf_op jit(solution)/shard_map/all_to_all | solution.py:873
  85.6 0.7 total.1
  (23 shorter events, 0.5 us)
Async XLA Ops:
  0.6 28.8 %copy-start.2 = (f32[19,4,8,128]{3,2,1,0:T(8,128)S(1)}, f32[19,4,8,128]{3,2,1,0:T(8,128)}, u32[]{:S(2)}) copy-start(f32[19,4,8,128]{3,2,1,0:T(8,128)} %pops.5) | copy-start | bytes 933892
  0.6 28.8 %copy-start.3 = (f32[19,4,8,128]{3,2,1,0:T(8,128)S(1)}, f32[19,4,8,128]{3,2,1,0:T(8,128)}, u32[]{:S(2)}) copy-start(f32[19,4,8,128]{3,2,1,0:T(8,128)} %seed.1) | copy-start | bytes 933892
  2.7 24.2 %collective-permute-start = (f32[65,8,128]{2,1,0:T(8,128)S(1)}, f32[65,8,128]{2,1,0:T(8,128)S(1)}, u32[]{:S(2)}, u32[]{:S(2)}) collective-permute-start(f32[65,8,128]{2,1,0:T(8,128)S(1)} %get-tuple-element.25), channel_id=1, source_target_pairs={{0,31},{1,0},{2,1},{3,2},{4,3},{5,4},{6,5},{7,6},{8,7},{9,8},{10,9... | collective-permute-start | bytes 798728 | tf_op jit(solution)/shard_map/ppermute | solution.py:782
  4.9 21.9 %collective-permute-start.1 = (f32[65,8,128]{2,1,0:T(8,128)S(1)}, f32[65,8,128]{2,1,0:T(8,128)S(1)}, u32[]{:S(2)}, u32[]{:S(2)}) collective-permute-start(f32[65,8,128]{2,1,0:T(8,128)S(1)} %get-tuple-element.26), channel_id=1, source_target_pairs={{0,1},{1,2},{2,3},{3,4},{4,5},{5,6},{6,7},{7,8},{8,9},{9,10},{10,1... | collective-permute-start | bytes 798728 | tf_op jit(solution)/shard_map/ppermute | solution.py:781
  28.9 8.7 %collective-permute-start.5 = (f32[24,1024]{1,0:T(8,128)S(1)}, f32[24,1024]{1,0:T(8,128)S(1)}, u32[]{:S(2)}, u32[]{:S(2)}) collective-permute-start(f32[24,1024]{1,0:T(8,128)S(1)} %push.1.lists), channel_id=1, source_target_pairs={{0,224},{32,0},{64,32},{96,64},{128,96},{160,128},{192,160},{224,1... | collective-permute-start | bytes 294920 | tf_op jit(solution)/shard_map/ppermute | solution.py:788
  29.1 8.5 %collective-permute-start.4 = (f32[24,1024]{1,0:T(8,128)S(1)}, f32[24,1024]{1,0:T(8,128)S(1)}, u32[]{:S(2)}, u32[]{:S(2)}) collective-permute-start(f32[24,1024]{1,0:T(8,128)S(1)} %push.1.lists), channel_id=1, source_target_pairs={{0,32},{32,64},{64,96},{96,128},{128,160},{160,192},{192,224},{224... | collective-permute-start | bytes 294920 | tf_op jit(solution)/shard_map/ppermute | solution.py:787
  29.6 16.4 %collective-permute-start.2 = (f32[228,8,128]{2,1,0:T(8,128)S(1)}, f32[228,8,128]{2,1,0:T(8,128)S(1)}, u32[]{:S(2)}, u32[]{:S(2)}) collective-permute-start(f32[228,8,128]{2,1,0:T(8,128)S(1)} %get-tuple-element.27.right_msg), channel_id=1, source_target_pairs={{0,32},{32,64},{64,96},{96,128},{128,160},{160,192},{192,224},{224... | collective-permute-start | bytes 2801672 | tf_op jit(solution)/shard_map/ppermute | solution.py:792
  30.7 15.2 %collective-permute-start.3 = (f32[228,8,128]{2,1,0:T(8,128)S(1)}, f32[228,8,128]{2,1,0:T(8,128)S(1)}, u32[]{:S(2)}, u32[]{:S(2)}) collective-permute-start(f32[228,8,128]{2,1,0:T(8,128)S(1)} %get-tuple-element.28.left_msg), channel_id=1, source_target_pairs={{0,224},{32,0},{64,32},{96,64},{128,96},{160,128},{192,160},{224,1... | collective-permute-start | bytes 2801672 | tf_op jit(solution)/shard_map/ppermute | solution.py:793
  37.7 26.9 %copy-start = (f32[4,18,4,16,128]{4,3,2,1,0:T(8,128)}, f32[4,18,4,16,128]{4,3,2,1,0:T(8,128)S(1)}, u32[]{:S(2)}) copy-start(f32[4,18,4,16,128]{4,3,2,1,0:T(8,128)S(1)} %get-tuple-element.32.s_own) | copy-start | bytes 7077892
  51.7 6.4 %collective-permute-start.6 = (f32[19,8,128]{2,1,0:T(8,128)S(1)}, f32[19,8,128]{2,1,0:T(8,128)S(1)}, u32[]{:S(2)}, u32[]{:S(2)}) collective-permute-start(f32[19,8,128]{2,1,0:T(8,128)S(1)} %get-tuple-element.37), channel_id=1, source_target_pairs={{0,31},{1,0},{2,1},{3,2},{4,3},{5,4},{6,5},{7,6},{8,7},{9,8},{10,9... | collective-permute-start | bytes 233480 | tf_op jit(solution)/shard_map/ppermute | solution.py:828
  53.2 4.9 %collective-permute-start.7 = (f32[19,8,128]{2,1,0:T(8,128)S(1)}, f32[19,8,128]{2,1,0:T(8,128)S(1)}, u32[]{:S(2)}, u32[]{:S(2)}) collective-permute-start(f32[19,8,128]{2,1,0:T(8,128)S(1)} %get-tuple-element.38), channel_id=1, source_target_pairs={{0,1},{1,2},{2,3},{3,4},{4,5},{5,6},{6,7},{7,8},{8,9},{9,10},{10,1... | collective-permute-start | bytes 233480 | tf_op jit(solution)/shard_map/ppermute | solution.py:827
  58.2 6.3 %collective-permute-start.8 = (f32[48,8,128]{2,1,0:T(8,128)S(1)}, f32[48,8,128]{2,1,0:T(8,128)S(1)}, u32[]{:S(2)}, u32[]{:S(2)}) collective-permute-start(f32[48,8,128]{2,1,0:T(8,128)S(1)} %get-tuple-element.41.right_msg), channel_id=1, source_target_pairs={{0,32},{32,64},{64,96},{96,128},{128,160},{160,192},{192,224},{224... | collective-permute-start | bytes 589832 | tf_op jit(solution)/shard_map/ppermute | solution.py:840
  58.2 6.3 %collective-permute-start.9 = (f32[48,8,128]{2,1,0:T(8,128)S(1)}, f32[48,8,128]{2,1,0:T(8,128)S(1)}, u32[]{:S(2)}, u32[]{:S(2)}) collective-permute-start(f32[48,8,128]{2,1,0:T(8,128)S(1)} %get-tuple-element.42.left_msg), channel_id=1, source_target_pairs={{0,224},{32,0},{64,32},{96,64},{128,96},{160,128},{192,160},{224,1... | collective-permute-start | bytes 589832 | tf_op jit(solution)/shard_map/ppermute | solution.py:841
  67.7 0.9 %copy-start.4 = (f32[19,6,16,128]{3,2,1,0:T(8,128)}, f32[19,6,16,128]{3,2,1,0:T(8,128)S(1)}, u32[]{:S(2)}) copy-start(f32[19,6,16,128]{3,2,1,0:T(8,128)S(1)} %get-tuple-element.46.a1) | copy-start | bytes 2801668
  68.6 17.0 %all-to-all-start.1 = ((f32[32,1,192]{2,1,0:T(1,128)}), f32[32,1,192]{2,1,0:T(1,128)S(1)}, u32[]{:S(2)}, u32[]{:S(2)}) async-start(f32[32,1,192]{2,1,0:T(1,128)} %get-tuple-element.47), calls=%async_computation.1 | async-start | bytes 65536 | tf_op jit(solution)/shard_map/all_to_all | solution.py:873
  77.0 1.7 %copy-start.1 = (f32[4,18,4,16,128]{4,3,2,1,0:T(8,128)S(1)}, f32[4,18,4,16,128]{4,3,2,1,0:T(8,128)}, u32[]{:S(2)}) copy-start(f32[4,18,4,16,128]{4,3,2,1,0:T(8,128)} %copy-done) | copy-start | bytes 7077892
  78.6 1.2 %copy-start.5 = (f32[19,6,16,128]{3,2,1,0:T(8,128)S(1)}, f32[19,6,16,128]{3,2,1,0:T(8,128)}, u32[]{:S(2)}) copy-start(f32[19,6,16,128]{3,2,1,0:T(8,128)} %copy-done.4) | copy-start | bytes 2801668

commit v2 on v1

--- a/solution.py
+++ b/solution.py
@@ -31,12 +31,14 @@
 OMEGA = 1.6
 F32 = jnp.float32
 BF16 = jnp.bfloat16
+F8 = jnp.float8_e4m3fn
 EXACT = lax.Precision.HIGHEST
 
 POP_TILES = 152
 SEED_TILES = 76
 LIST_TILES = 8
-X_TILES = POP_TILES + SEED_TILES
+FAR_POPS, NEAR_SEED, FAR_SEED, X_TILES = 114, 124, 162, 172
+OUTWARD = tuple(tuple(q for q in range(19) if VELOCITIES[q][0] == c) for c in (-1, 1))
 Y_TILES = 38 + 19 + LIST_TILES
 SIDE_COUNT = (3, 2, 1, 1)
 SIDE_BASE = (0, 3, 5, 6)
@@ -161,8 +163,7 @@
     speeds = jnp.concatenate([owned[:, 64 * c : 64 * c + 64] for c in range(3)], axis=0)
     high = speeds.astype(BF16)
     rest = (speeds - high.astype(F32)).astype(BF16)
-    last = (speeds - high.astype(F32) - rest.astype(F32)).astype(BF16)
-    pieces = jnp.concatenate([high, rest, last], axis=0)
+    pieces = jnp.concatenate([high, rest], axis=0)
     iota = iota256()
     owner_iota = row_iota((32, 1024)).astype(F32)
     for k, table8 in enumerate((lists[...], read_list(from_up, 57), read_list(from_down, 57))):
@@ -172,7 +173,7 @@
             owner = jnp.floor(slot * (1.0 / 64.0))
             place = slot - owner * 64.0
             picked = jnp.dot(pieces, onehot(place, 64, iota), preferred_element_type=F32)
-            picked = picked[:96] + picked[96:192] + picked[192:]
+            picked = picked[:96] + picked[96:]
             match = owner_iota == owner
             opposite = table8[s : s + 1, :].astype(jnp.int32) // 4096
             push = jnp.zeros((1, 1024), F32)
@@ -184,29 +185,43 @@
             out[8 * k + 4 + s : 8 * k + 5 + s, :] = push
 
 
-def pack_kernel(pops, seed, from_up, from_down, right_msg, left_msg):
-    low = low_half((8, 128))
-    sub = row_iota((8, 128))
+def extended(pops, seed, from_up, from_down, low, sub):
     for q in range(19):
         for i in range(2):
             up = from_up[2 * q + i]
             down = from_down[2 * q + i]
-            even = jnp.where(low, up, down)
+            yield 0, q, 2 * i, pops[q, 2 * i], jnp.where(low, up, down)
             odd = pltpu.roll(jnp.where(low, down, up), 4, 0)
-            for x, halo in ((2 * i, even), (2 * i + 1, odd)):
-                k = (q * 4 + x) * 2
-                own = pops[q, x]
-                for msg in (right_msg, left_msg):
-                    msg[k] = own
-                    msg[k + 1] = halo
-        up = from_up[38 + q]
-        down = from_down[38 + q]
+            yield 0, q, 2 * i + 1, pops[q, 2 * i + 1], odd
         for x in range(4):
-            halo = widen_two(up, down, x, sub)
-            msg = left_msg if x < 2 else right_msg
-            k = POP_TILES + (q * 2 + x % 2) * 2
-            msg[k] = seed[q, x]
+            yield 1, q, x, seed[q, x], widen_two(from_up[38 + q], from_down[38 + q], x, sub)
+
+
+def pack_kernel(pops, seed, from_up, from_down, right_msg, left_msg, edge):
+    low = low_half((8, 128))
+    sub = row_iota((8, 128))
+    for kind, q, x, own, halo in extended(pops, seed, from_up, from_down, low, sub):
+        places = []
+        if kind == 0:
+            if x >= 1:
+                places.append((right_msg, (q * 3 + x - 1) * 2))
+            if x <= 2:
+                places.append((left_msg, (q * 3 + x) * 2))
+            if x in (0, 3):
+                places.append((edge, (q * 2 + x // 3) * 2))
+        elif x in (0, 3):
+            places.append((left_msg if x == 0 else right_msg, NEAR_SEED + 2 * q))
+        elif q in OUTWARD[2 - x]:
+            side = left_msg if x == 1 else right_msg
+            places.append((side, FAR_SEED + 2 * OUTWARD[2 - x].index(q)))
+        for msg, k in places:
+            msg[k] = own
             msg[k + 1] = halo
+    for msg, x, moving in ((right_msg, 0, OUTWARD[1]), (left_msg, 1, OUTWARD[0])):
+        g, _ = collide_column([ext(edge, (q * 2 + x) * 2) for q in range(19)])
+        for i, q in enumerate(moving):
+            msg[FAR_POPS + 2 * i] = g[q][:8]
+            msg[FAR_POPS + 2 * i + 1] = g[q][8:]
 
 
 def widen_two(up, down, x, sub):
@@ -263,9 +278,12 @@
         outside = outside | (y < 4)
     target = onehot(jnp.where(outside, -1, row).astype(F32), rows, iota)
     zcode = z.astype(F32).astype(BF16)
-    high = push.astype(BF16)
-    mid = (push - high.astype(F32)).astype(BF16)
-    last = (push - high.astype(F32) - mid.astype(F32)).astype(BF16)
+    scaled = push * 256.0
+    high = scaled.astype(F8).astype(BF16)
+    scaled = (scaled - high.astype(F32)) * 16.0
+    mid = scaled.astype(F8).astype(BF16)
+    scaled = (scaled - mid.astype(F32)) * 16.0
+    last = scaled.astype(F8).astype(BF16)
     zero = jnp.array(0.0, BF16)
     blocks = [[], [], [], []]
     for t in range(8):
@@ -276,9 +294,14 @@
             b.append(jnp.where(match, piece[:, cut], zero))
     values = jnp.concatenate([jnp.concatenate(b, axis=1) for b in blocks], axis=0)
     dense = lax.dot_general(
-        target, values, (((1,), (1,)), ((), ())), preferred_element_type=F32
+        target.astype(F8), values.astype(F8), (((1,), (1,)), ((), ())), preferred_element_type=F32
     )[:rows]
-    return dense[:, :128], dense[:, 128:256] + dense[:, 256:384] + dense[:, 384:]
+    total = (
+        dense[:, 128:256] * (1.0 / 256.0)
+        + dense[:, 256:384] * (1.0 / 4096.0)
+        + dense[:, 384:] * (1.0 / 65536.0)
+    )
+    return dense[:, :128], total
 
 
 def scatter_columns(lists, s, index, first, count, iota, n_ref, s_ref, where):
@@ -468,10 +491,12 @@
 
 
 def window_kernel(
-    right_msg,
-    left_msg,
-    from_left,
-    from_right,
+    pops,
+    seed,
+    from_up,
+    from_down,
+    left_hbm,
+    right_hbm,
     n_own,
     s_own,
     n_side,
@@ -487,16 +512,40 @@
     f3,
     a4,
     a3,
+    own_pops,
+    from_left,
+    from_right,
+    sems,
 ):
     def groups(s):
         return column_groups(s, n_own, s_own, n_side, s_side)
 
-    for ref, start in ((from_left, 0), (right_msg, 4), (from_right, 8)):
-
-        def load(q, i, ref=ref):
-            return ref[pl.ds((q * 4 + i) * 2, 2)].reshape(16, 128)
-
-        collide_into(load, start, 4, relaxed, density)
+    copies = [
+        pltpu.make_async_copy(left_hbm, from_left, sems.at[0]),
+        pltpu.make_async_copy(right_hbm, from_right, sems.at[1]),
+    ]
+    for copy in copies:
+        copy.start()
+    low = low_half((8, 128))
+    for kind, q, x, own, halo in extended(pops, seed, from_up, from_down, low, row_iota((8, 128))):
+        if kind == 0:
+            own_pops[(q * 4 + x) * 2] = own
+            own_pops[(q * 4 + x) * 2 + 1] = halo
+        else:
+            a4[q, 4 + x, 0:8] = own
+            a4[q, 4 + x, 8:16] = halo
+    for ref, start, count in ((own_pops, 4, 4), (from_left, 1, 3), (from_right, 8, 3)):
+        if start == 1:
+            for copy in copies:
+                copy.wait()
+
+        def load(q, i, ref=ref, count=count):
+            return ref[pl.ds((q * count + i) * 2, 2)].reshape(16, 128)
+
+        collide_into(load, start, count, relaxed, density)
+    for i in range(5):
+        relaxed[OUTWARD[1][i], 0] = ext(from_left, FAR_POPS + 2 * i)
+        relaxed[OUTWARD[0][i], 11] = ext(from_right, FAR_POPS + 2 * i)
     stream_into(relaxed, density, groups(0), f2)
     for q in range(19):
         f1_out[q] = f2[q, 3:9]
@@ -505,12 +554,11 @@
     collide_into(lambda q, i: f2[q, 2 + i], 2, 8, relaxed, density)
     stream_into(relaxed, density, groups(2), f3)
     for q in range(19):
-        for x in range(2):
-            k = POP_TILES + (q * 2 + x) * 2
-            a4[q, 2 + x] = ext(from_left, k)
-            a4[q, 4 + x] = ext(left_msg, k)
-            a4[q, 6 + x] = ext(right_msg, k)
-            a4[q, 8 + x] = ext(from_right, k)
+        a4[q, 3] = ext(from_left, NEAR_SEED + 2 * q)
+        a4[q, 8] = ext(from_right, NEAR_SEED + 2 * q)
+    for i in range(5):
+        a4[OUTWARD[0][i], 2] = ext(from_left, FAR_SEED + 2 * i)
+        a4[OUTWARD[1][i], 9] = ext(from_right, FAR_SEED + 2 * i)
     for start, count, counts, pushes in groups(3):
 
         def third(i, carry, start=start, count=count, counts=counts, pushes=pushes):
@@ -556,7 +604,6 @@
         down_msg[q], up_msg[q] = edge_rows([a2_out[q, x] for x in range(4)], pair)
 
 
-OUTWARD = tuple(tuple(q for q in range(19) if VELOCITIES[q][0] == c) for c in (-1, 1))
 A_TILES = 48
 
 
@@ -604,18 +651,21 @@
         )
         slot = lists[4 + s : 5 + s, :].astype(jnp.int32)
         opposite = code.astype(jnp.int32) // 4096
-        owner = jnp.where(row_iota((32, 1024)) == slot // 64, 1.0, 0.0)
+        owner = onehot((slot // 64).astype(F32), 32, iota)
         place = row_iota((64, 1024)) == slot % 64
         parts = jnp.concatenate(
             [jnp.where(place, -value * signs(opposite, c), 0.0) for c in range(3)], axis=0
         )
-        total = total + lax.dot_general(
+        high = parts.astype(BF16)
+        rest = (parts - high.astype(F32)).astype(BF16)
+        low = (parts - high.astype(F32) - rest.astype(F32)).astype(BF16)
+        summed = lax.dot_general(
             owner,
-            parts,
+            jnp.concatenate([high, rest, low], axis=0),
             (((1,), (1,)), ((), ())),
-            precision=EXACT,
             preferred_element_type=F32,
         )
+        total = total + (summed[:, :192] + summed[:, 192:384] + summed[:, 384:])
     return total
 
 
@@ -642,10 +692,12 @@
     s_side,
     late,
     lists,
+    a1_out,
+    grad_out,
     a1,
-    grad_out,
     a2,
     pull,
+    sem,
 ):
     for q in range(19):
         a2[q, 1] = ext(from_left, 2 * q)
@@ -679,8 +731,11 @@
             return carry
 
         lax.fori_loop(0, count, first, 0)
+    copy = pltpu.make_async_copy(a1, a1_out, sem.at[0])
+    copy.start()
     total = late[...] + link_gradient([pull[...].reshape(576, 128)], lists, (0,))
     grad_out[...] = total.reshape(32, 1, 192)
+    copy.wait()
 
 
 def total_kernel(parts, out):
@@ -757,7 +812,7 @@
         link_node,
         node_slot.reshape(128, 128),
     )
-    up_msg, down_msg, lists, copies = pl.pallas_call(
+    up_msg, down_msg, lists, copies, pops, seed = pl.pallas_call(
         front_kernel,
         name="front",
         out_shape=[
@@ -765,10 +820,12 @@
             shape(Y_TILES, 8, 128),
             shape(8, 1024),
             shape(32, 1, 192),
+            shape(19, 4, 8, 128),
+            shape(19, 4, 8, 128),
         ],
         in_specs=[smem] + [pl.BlockSpec(memory_space=pltpu.HBM)] * 8,
-        out_specs=[full()] * 4,
-        scratch_shapes=[pltpu.VMEM(a.shape, a.dtype) for a in operands]
+        out_specs=[full()] * 6,
+        scratch_shapes=[pltpu.VMEM(a.shape, a.dtype) for a in operands[2:]]
         + [pltpu.SMEM((4,), jnp.int32), pltpu.SemaphoreType.DMA((8,))],
         compiler_params=pltpu.CompilerParams(vmem_limit_bytes=12 << 20),
     )(
@@ -781,24 +838,30 @@
     from_down = lax.ppermute(up_msg, "gy", ring("gy", 1))
     from_up = lax.ppermute(down_msg, "gy", ring("gy", -1))
     wall = lax.all_to_all(copies, "gy", split_axis=0, concat_axis=0, tiled=True)
+    right_msg, left_msg = call(
+        pack_kernel,
+        "pack",
+        [shape(X_TILES, 8, 128)] * 2,
+        4,
+        8,
+        [pltpu.VMEM((SEED_TILES, 8, 128), F32)],
+    )(pops, seed, from_up, from_down)
+    lists, right_msg, left_msg = lax.optimization_barrier((lists, right_msg, left_msg))
+    from_left = lax.ppermute(right_msg, "gx", ring("gx", 1))
+    from_right = lax.ppermute(left_msg, "gx", ring("gx", -1))
     all_lists = call(push_kernel, "push", shape(24, 1024), 4, 8, flops=500_000_000, moved=500_000)(
         wall, lists, from_up, from_down
     )
     left_lists = lax.ppermute(all_lists, "gx", ring("gx", 1))
     right_lists = lax.ppermute(all_lists, "gx", ring("gx", -1))
-    right_msg, left_msg = call(pack_kernel, "pack", [shape(X_TILES, 8, 128)] * 2, 4, 8)(
-        populations, adjoint_seed, from_up, from_down
-    )
-    from_left = lax.ppermute(right_msg, "gx", ring("gx", 1))
-    from_right = lax.ppermute(left_msg, "gx", ring("gx", -1))
     n_own, s_own = call(
         own_links_kernel,
         "own_links",
         [shape(4, 18, 4, 16, 128)] * 2,
         1,
         24,
-        flops=5_000_000_000,
-        moved=5_000_000,
+        flops=3_500_000_000,
+        moved=1_000_000,
     )(all_lists)
     n_side, s_side = call(
         side_links_kernel,
@@ -806,24 +869,27 @@
         [shape(2, 18, 7, 16, 128)] * 2,
         2,
         24,
-        flops=5_000_000_000,
-        moved=5_000_000,
+        flops=3_500_000_000,
+        moved=1_000_000,
     )(left_lists, right_lists)
     region = pltpu.VMEM((19, 12, 16, 128), F32)
-    f1, a2, up_msg, down_msg, pull = call(
+    arrived = pltpu.VMEM((X_TILES, 8, 128), F32)
+    f1, a2, up_msg, down_msg, pull = pl.pallas_call(
         window_kernel,
-        "window",
-        [
+        name="window",
+        out_shape=[
             shape(19, 6, 16, 128),
             shape(19, 4, 8, 128),
             shape(19, 8, 128),
             shape(19, 8, 128),
             shape(3, 18, 4, 8, 128),
         ],
-        8,
-        30,
-        [region, pltpu.VMEM((12, 16, 128), F32), region, region, region, region],
-    )(right_msg, left_msg, from_left, from_right, n_own, s_own, n_side, s_side)
+        in_specs=[full()] * 4 + [pl.BlockSpec(memory_space=pl.ANY)] * 2 + [full()] * 4,
+        out_specs=[full()] * 5,
+        scratch_shapes=[region, pltpu.VMEM((12, 16, 128), F32), region, region, region, region]
+        + [pltpu.VMEM((POP_TILES, 8, 128), F32), arrived, arrived, pltpu.SemaphoreType.DMA((2,))],
+        compiler_params=pltpu.CompilerParams(vmem_limit_bytes=32 << 20),
+    )(pops, seed, from_up, from_down, from_left, from_right, n_own, s_own, n_side, s_side)
     from_down = lax.ppermute(up_msg, "gy", ring("gy", 1))
     from_up = lax.ppermute(down_msg, "gy", ring("gy", -1))
     late = call(
@@ -848,20 +914,26 @@
         flops=1_000_000_000,
         moved=1_000_000,
     )(pull, lists, late)
-    a1, owned = call(
+    a1, owned = pl.pallas_call(
         first_adjoint_kernel,
-        "first_adjoint",
-        [shape(19, 6, 16, 128), shape(32, 1, 192)],
-        13,
-        24,
-        [pltpu.VMEM((19, 8, 16, 128), F32), pltpu.VMEM((18, 4, 8, 128), F32)],
+        name="first_adjoint",
+        out_shape=[pltpu.HBM((19, 6, 16, 128), F32), shape(32, 1, 192)],
+        in_specs=[full()] * 13,
+        out_specs=[pl.BlockSpec(memory_space=pltpu.HBM), full()],
+        scratch_shapes=[
+            pltpu.VMEM((19, 6, 16, 128), F32),
+            pltpu.VMEM((19, 8, 16, 128), F32),
+            pltpu.VMEM((18, 4, 8, 128), F32),
+            pltpu.SemaphoreType.DMA((1,)),
+        ],
+        compiler_params=pltpu.CompilerParams(vmem_limit_bytes=24 << 20),
     )(
         right_msg,
         left_msg,
         middle,
         from_left,
         from_right,
-        populations,
+        pops,
         f1,
         n_own,
         s_own,
@@ -879,7 +951,7 @@
         12,
         flops=10_000_000,
         moved=4_000_000,
-    )(a1, populations, n_own, s_own)
+    )(a1, pops, n_own, s_own)
     gradient = call(total_kernel, "total", shape(3, 64), 1, 4)(arrived)
     return (adjoint, gradient)
 

time: 86.9 us -> 81.9 us (0.942)
  blocking collectives: 21.9 us -> 0 us
  starting transfers between devices: 19.1 us -> 34.3 us
  waiting for transfers between devices: 6.18 us -> 15.5 us
  Pallas kernels: 34.5 us -> 27.6 us
  local copies, waits for them, and re-layouts: 3.79 us -> 2.85 us
    all_to_all x1 -> x0, blocking collectives: 21.9 us -> none  [shards(): wall = lax.all_to_all(copies, 'gy', split_axis=0, concat_axis=0, tiled=True)]
    all_to_all x0 -> x1, starting transfers between devices: none -> 13.5 us  [shards(): wall = lax.all_to_all(copies, 'gy', split_axis=0, concat_axis=0, tiled=True)]
    all_to_all x0 -> x1, waiting for transfers between devices: none -> 4.43 us  [shards(): wall = lax.all_to_all(copies, 'gy', split_axis=0, concat_axis=0, tiled=True)]
    pallas_call x1, Pallas kernels: 8.26 us -> 4.33 us  [shards(): call(side_links_kernel, 'side_links', [shape(2, 18, 7, 16, 128)] * 2, 2,...]
    ppermute x2, waiting for transfers between devices: 0.01 us -> 2.2 us  [shards(): from_down = lax.ppermute(up_msg, 'gy', ring('gy', 1))]
    pallas_call x1, Pallas kernels: 5.1 us -> 2.93 us  [shards(): call(own_links_kernel, 'own_links', [shape(4, 18, 4, 16, 128)] * 2, 1, 24...]
    pallas_call x1, Pallas kernels: 4.26 us -> 2.14 us  [shards(): call(late_links_kernel, 'late_links', shape(32, 192), 2, 16, flops=200000...]
    pallas_call x3, Pallas kernels: 9.05 us -> 11.1 us  [the longest x1 6.41 us: shards(): pl.pallas_call(window_kernel, name='window', out_shape=[shape(19, 6, 16,...]
  transfers between devices with their start and end apart: 11 -> 12, of which waited for: 2 -> 7; matrix products, arithmetic and copies ran while one was open for 0% -> 0% of each run, Pallas kernels for 24% -> 18%
where the time goes in v2:
time: 81.9 us; the launch traced here: 80.9 us
  starting transfers between devices  34.3 us (42%)
  Pallas kernels  27.6 us (34%)
  waiting for transfers between devices  15.5 us (19%)
  local copies, waits for them, and re-layouts  2.85 us (3%)
    all_to_all x1, starting transfers between devices, shards(): wall = lax.all_to_all(copies, 'gy', split_axis=0, concat_axis=0, tiled=True)  13.5 us
    all_to_all x1, starting transfers between devices, shards(): lax.all_to_all(owned, 'gy', split_axis=0, concat_axis=0, tiled=True)  9.1 us
    pallas_call x1, Pallas kernels, shards(): pl.pallas_call(window_kernel, name='window', out_shape=[shape(19, 6, 16,...  6.41 us
    ppermute x2, starting transfers between devices, shards(): from_right = lax.ppermute(left_msg, 'gx', ring('gx', -1))  5.9 us
    ppermute x2, starting transfers between devices, shards(): from_up = lax.ppermute(down_msg, 'gy', ring('gy', -1))  5.24 us
    all_to_all x1, waiting for transfers between devices, shards(): lax.all_to_all(owned, 'gy', split_axis=0, concat_axis=0, tiled=True)  4.61 us
    all_to_all x1, waiting for transfers between devices, shards(): wall = lax.all_to_all(copies, 'gy', split_axis=0, concat_axis=0, tiled=True)  4.43 us
    pallas_call x1, Pallas kernels, shards(): call(side_links_kernel, 'side_links', [shape(2, 18, 7, 16, 128)] * 2, 2,...  4.33 us
  transfers between devices with their start and end apart: 12, of which 7 were waited for; matrix products, arithmetic and copies ran while one was open for 0% of the time, Pallas kernels for 18%

profile of v2, /device:TPU:8, one launch (start us, length us, event | category | flops | bytes accessed | tf_op | source)
XLA Modules:
  0.0 80.9 jit_solution(955084818898847222)
XLA Ops:
  0.6 2.5 %front.1 = (f32[65,8,128]{2,1,0:T(8,128)S(1)}, f32[65,8,128]{2,1,0:T(8,128)S(1)}, f32[8,1024]{1,0:T(8,128)S(1)}, f32[32,1,192]{2,1,0:T(1,128)}, f32[19,4,8,128]{...) custom-call(s32[1]{0:T(128)} %bitcast.base, s32[4]{0:T(128)} %bitcast.4, f32[19,4,8,128]{3,2,1,0:T(8,128)} %pops_hbm.1, ...), custom_call_target="tpu_custom_call" | custom-call | tf_op jit(solution)/shard_map/front/pallas_call | solution.py:815
  3.1 2.3 %collective-permute-start = (f32[65,8,128]{2,1,0:T(8,128)S(1)}, f32[65,8,128]{2,1,0:T(8,128)S(1)}, u32[]{:S(2)}, u32[]{:S(2)}) collective-permute-start(f32[65,8,128]{2,1,0:T(8,128)S(1)} %get-tuple-element.32), channel_id=1, source_target_pairs={{0,31},{1,0},{2,1},{3,2},{4,3},{5,4},{6,5},{7,6},{8,7},{9,8},{10,9... | collective-permute-start | bytes 798728 | tf_op jit(solution)/shard_map/ppermute | solution.py:839
  5.4 13.5 %all-to-all-start = ((f32[32,1,192]{2,1,0:T(1,128)}), f32[32,1,192]{2,1,0:T(1,128)S(1)}, u32[]{:S(2)}, u32[]{:S(2)}) async-start(f32[32,1,192]{2,1,0:T(1,128)} %get-tuple-element.39), calls=%async_computation | async-start | bytes 65536 | tf_op jit(solution)/shard_map/all_to_all | solution.py:840
  18.9 1.2 %pack.1 = (f32[172,8,128]{2,1,0:T(8,128)}, f32[172,8,128]{2,1,0:T(8,128)}) custom-call(f32[19,4,8,128]{3,2,1,0:T(8,128)S(1)} %get-tuple-element.30.pops, f32[19,4,8,128]{3,2,1,0:T(8,128)S(1)} %get-tuple-element.31.seed, f32[65,8,128]{2,1,0:T(8,128)S(1)} %collective-permute-done.from_up, f32[65,8,128]{2,1,0:T(8,128)S(1)} %collective-permute-done.1.from_down), custom_call_target="tpu_custom_call" | custom-call | tf_op jit(solution)/shard_map/pack/pallas_call | solution.py:841
  20.1 3.0 %collective-permute-start.3 = (f32[172,8,128]{2,1,0:T(8,128)}, f32[172,8,128]{2,1,0:T(8,128)}, u32[]{:S(2)}, u32[]{:S(2)}) collective-permute-start(f32[172,8,128]{2,1,0:T(8,128)} %get-tuple-element.38), channel_id=1, source_target_pairs={{0,224},{32,0},{64,32},{96,64},{128,96},{160,128},{192,160},{224,1... | collective-permute-start | bytes 2113544 | tf_op jit(solution)/shard_map/ppermute | solution.py:851
  23.1 4.4 %all-to-all-done.wall = f32[32,1,192]{2,1,0:T(1,128)S(1)} async-done(((f32[32,1,192]{2,1,0:T(1,128)}), f32[32,1,192]{2,1,0:T(1,128)S(1)}, u32[]{:S(2)}, u32[]{:S(2)}) %all-to-all-start) | async-done | bytes 24608 | tf_op jit(solution)/shard_map/all_to_all | solution.py:840
  27.5 1.5 %push.1.lists = f32[24,1024]{1,0:T(8,128)S(1)} custom-call(f32[32,1,192]{2,1,0:T(1,128)S(1)} %all-to-all-done.wall, f32[8,1024]{1,0:T(8,128)S(1)} %get-tuple-element.40.lists, f32[65,8,128]{2,1,0:T(8,128)S(1)} %collective-permute-done.from_up, f32[65,8,128]{2,1,0:T(8,128)S(1)} %collective-permute-done.1.from_down), custom_call_target="tpu_custom_call" | custom-call | flops 500000000 | bytes 500000 | tf_op jit(solution)/shard_map/push/pallas_call | solution.py:852
  29.6 2.9 %own_links.1 = (f32[4,18,4,16,128]{4,3,2,1,0:T(8,128)S(1)}, f32[4,18,4,16,128]{4,3,2,1,0:T(8,128)S(1)}) custom-call(f32[24,1024]{1,0:T(8,128)S(1)} %push.1.lists), custom_call_target="tpu_custom_call" | custom-call | flops 3500000000 | bytes 1000000 | tf_op jit(solution)/shard_map/own_links/pallas_call | solution.py:857
  33.0 1.5 %collective-permute-done.4.from_left = f32[24,1024]{1,0:T(8,128)S(1)} collective-permute-done((f32[24,1024]{1,0:T(8,128)S(1)}, f32[24,1024]{1,0:T(8,128)S(1)}, u32[]{:S(2)}, u32[]{:S(2)}) %collective-permute-start.4) | collective-permute-done | bytes 98336 | tf_op jit(solution)/shard_map/ppermute | solution.py:855
  34.5 4.3 %side_links.1 = (f32[2,18,7,16,128]{4,3,2,1,0:T(8,128)S(1)}, f32[2,18,7,16,128]{4,3,2,1,0:T(8,128)S(1)}) custom-call(f32[24,1024]{1,0:T(8,128)S(1)} %collective-permute-done.4.from_left, f32[24,1024]{1,0:T(8,128)S(1)} %collective-permute-done.5.from_right), custom_call_target="tpu_custom_call" | custom-call | flops 3500000000 | bytes 1000000 | tf_op jit(solution)/shard_map/side_links/pallas_call | solution.py:866
  38.9 6.4 %window.1 = (f32[19,6,16,128]{3,2,1,0:T(8,128)S(1)}, f32[19,4,8,128]{3,2,1,0:T(8,128)S(1)}, f32[19,8,128]{2,1,0:T(8,128)S(1)}, f32[19,8,128]{2,1,0:T(8,128)S(1)}, f32[3,18,4,8,128]{4,3,2,1,0:T(8,128)S(1)}) custom-call(f32[19,4,8,128]{3,2,1,0:T(8,128)S(1)} %get-tuple-element.30.pops, f32[19,4,8,128]{3,2,1,0:T(8,128)S(1)} %get-tuple-element.31.seed, ...), custom_call_target="tpu_custom_call" | custom-call | tf_op jit(solution)/shard_map/window/pallas_call | solution.py:877
  45.3 3.0 %collective-permute-start.6 = (f32[19,8,128]{2,1,0:T(8,128)S(1)}, f32[19,8,128]{2,1,0:T(8,128)S(1)}, u32[]{:S(2)}, u32[]{:S(2)}) collective-permute-start(f32[19,8,128]{2,1,0:T(8,128)S(1)} %get-tuple-element.47), channel_id=1, source_target_pairs={{0,31},{1,0},{2,1},{3,2},{4,3},{5,4},{6,5},{7,6},{8,7},{9,8},{10,9... | collective-permute-start | bytes 233480 | tf_op jit(solution)/shard_map/ppermute | solution.py:894
  48.3 2.1 %late_links.1.late = f32[32,192]{1,0:T(8,128)S(1)} custom-call(f32[3,18,4,8,128]{4,3,2,1,0:T(8,128)S(1)} %get-tuple-element.46.pull, f32[8,1024]{1,0:T(8,128)S(1)} %get-tuple-element.40.lists), custom_call_target="tpu_custom_call" | custom-call | flops 2000000000 | bytes 2000000 | tf_op jit(solution)/shard_map/late_links/pallas_call | solution.py:895
  50.5 2.2 %collective-permute-done.7.from_down = f32[19,8,128]{2,1,0:T(8,128)S(1)} collective-permute-done((f32[19,8,128]{2,1,0:T(8,128)S(1)}, f32[19,8,128]{2,1,0:T(8,128)S(1)}, u32[]{:S(2)}, u32[]{:S(2)}) %collective-permute-start.7) | collective-permute-done | bytes 77856 | tf_op jit(solution)/shard_map/ppermute | solution.py:893
  52.8 2.9 %collective-permute-start.9 = (f32[48,8,128]{2,1,0:T(8,128)S(1)}, f32[48,8,128]{2,1,0:T(8,128)S(1)}, u32[]{:S(2)}, u32[]{:S(2)}) collective-permute-start(f32[48,8,128]{2,1,0:T(8,128)S(1)} %get-tuple-element.52.left_msg), channel_id=1, source_target_pairs={{0,224},{32,0},{64,32},{96,64},{128,96},{160,128},{192,160},{224,1... | collective-permute-start | bytes 589832 | tf_op jit(solution)/shard_map/ppermute | solution.py:907
  55.7 1.2 %early_links.1.late = f32[32,192]{1,0:T(8,128)S(1)} custom-call(f32[3,18,4,8,128]{4,3,2,1,0:T(8,128)S(1)} %get-tuple-element.46.pull, f32[8,1024]{1,0:T(8,128)S(1)} %get-tuple-element.40.lists, f32[32,192]{1,0:T(8,128)S(1)} %late_links.1.late), custom_call_target="tpu_custom_call" | custom-call | flops 1000000000 | bytes 1000000 | tf_op jit(solution)/shard_map/early_links/pallas_call | solution.py:908
  56.9 2.2 %collective-permute-done.8.from_left = f32[48,8,128]{2,1,0:T(8,128)S(1)} collective-permute-done((f32[48,8,128]{2,1,0:T(8,128)S(1)}, f32[48,8,128]{2,1,0:T(8,128)S(1)}, u32[]{:S(2)}, u32[]{:S(2)}) %collective-permute-start.8) | collective-permute-done | bytes 196640 | tf_op jit(solution)/shard_map/ppermute | solution.py:906
  59.1 3.5 %first_adjoint.1 = (f32[19,6,16,128]{3,2,1,0:T(8,128)}, f32[32,1,192]{2,1,0:T(1,128)}) custom-call(f32[48,8,128]{2,1,0:T(8,128)S(1)} %get-tuple-element.51.right_msg, f32[48,8,128]{2,1,0:T(8,128)S(1)} %get-tuple-element.52.left_msg, f32[76,8,128]{2,1,0:T(8,128)S(1)} %get-tuple-element.53.middle, f32[48,8,128]{2,1,0:T(8,128)S(1)} %collective-permute-done.8.from_left, ...), custom_call_target="tpu_custom_call" | custom-call | tf_op jit(solution)/shard_map/first_adjoint/pallas_call | solution.py:917
  62.5 9.1 %all-to-all-start.1 = ((f32[32,1,192]{2,1,0:T(1,128)}), f32[32,1,192]{2,1,0:T(1,128)S(1)}, u32[]{:S(2)}, u32[]{:S(2)}) async-start(f32[32,1,192]{2,1,0:T(1,128)} %get-tuple-element.57), calls=%async_computation.1 | async-start | bytes 65536 | tf_op jit(solution)/shard_map/all_to_all | solution.py:945
  71.7 1.7 %copy-done.1 = f32[4,18,4,16,128]{4,3,2,1,0:T(8,128)S(1)} copy-done((f32[4,18,4,16,128]{4,3,2,1,0:T(8,128)S(1)}, f32[4,18,4,16,128]{4,3,2,1,0:T(8,128)}, u32[]{:S(2)}) %copy-start.1) | copy-done | bytes 2359320
  73.3 1.2 %copy-done.2 = f32[19,6,16,128]{3,2,1,0:T(8,128)S(1)} copy-done((f32[19,6,16,128]{3,2,1,0:T(8,128)S(1)}, f32[19,6,16,128]{3,2,1,0:T(8,128)}, u32[]{:S(2)}) %copy-start.2) | copy-done | bytes 933912
  74.5 1.2 %last_adjoint.1 = f32[19,4,8,128]{3,2,1,0:T(8,128)} custom-call(f32[19,6,16,128]{3,2,1,0:T(8,128)S(1)} %copy-done.2, f32[19,4,8,128]{3,2,1,0:T(8,128)S(1)} %get-tuple-element.30.pops, f32[4,18,4,16,128]{4,3,2,1,0:T(8,128)S(1)} %get-tuple-element.41.n_own, f32[4,18,4,16,128]{4,3,2,1,0:T(8,128)S(1)} %copy-done.1), custom_call_target="tpu_custom_call" | custom-call | flops 10000000 | bytes 4000000 | tf_op jit(solution)/shard_map/last_adjoint/pallas_call | solution.py:946
  75.6 4.6 %all-to-all-done.1.parts = f32[32,1,192]{2,1,0:T(1,128)S(1)} async-done(((f32[32,1,192]{2,1,0:T(1,128)}), f32[32,1,192]{2,1,0:T(1,128)S(1)}, u32[]{:S(2)}, u32[]{:S(2)}) %all-to-all-start.1) | async-done | bytes 24608 | tf_op jit(solution)/shard_map/all_to_all | solution.py:945
  80.3 0.7 total.1
  (18 shorter events, 1.1 us)
Async XLA Ops:
  3.1 15.8 %collective-permute-start = (f32[65,8,128]{2,1,0:T(8,128)S(1)}, f32[65,8,128]{2,1,0:T(8,128)S(1)}, u32[]{:S(2)}, u32[]{:S(2)}) collective-permute-start(f32[65,8,128]{2,1,0:T(8,128)S(1)} %get-tuple-element.32), channel_id=1, source_target_pairs={{0,31},{1,0},{2,1},{3,2},{4,3},{5,4},{6,5},{7,6},{8,7},{9,8},{10,9... | collective-permute-start | bytes 798728 | tf_op jit(solution)/shard_map/ppermute | solution.py:839
  5.4 13.5 %collective-permute-start.1 = (f32[65,8,128]{2,1,0:T(8,128)S(1)}, f32[65,8,128]{2,1,0:T(8,128)S(1)}, u32[]{:S(2)}, u32[]{:S(2)}) collective-permute-start(f32[65,8,128]{2,1,0:T(8,128)S(1)} %get-tuple-element.33), channel_id=1, source_target_pairs={{0,1},{1,2},{2,3},{3,4},{4,5},{5,6},{6,7},{7,8},{8,9},{9,10},{10,1... | collective-permute-start | bytes 798728 | tf_op jit(solution)/shard_map/ppermute | solution.py:838
  5.4 22.1 %all-to-all-start = ((f32[32,1,192]{2,1,0:T(1,128)}), f32[32,1,192]{2,1,0:T(1,128)S(1)}, u32[]{:S(2)}, u32[]{:S(2)}) async-start(f32[32,1,192]{2,1,0:T(1,128)} %get-tuple-element.39), calls=%async_computation | async-start | bytes 65536 | tf_op jit(solution)/shard_map/all_to_all | solution.py:840
  20.1 18.7 %collective-permute-start.2 = (f32[172,8,128]{2,1,0:T(8,128)}, f32[172,8,128]{2,1,0:T(8,128)}, u32[]{:S(2)}, u32[]{:S(2)}) collective-permute-start(f32[172,8,128]{2,1,0:T(8,128)} %get-tuple-element.37), channel_id=1, source_target_pairs={{0,32},{32,64},{64,96},{96,128},{128,160},{160,192},{192,224},{224... | collective-permute-start | bytes 2113544 | tf_op jit(solution)/shard_map/ppermute | solution.py:850
  20.1 18.7 %collective-permute-start.3 = (f32[172,8,128]{2,1,0:T(8,128)}, f32[172,8,128]{2,1,0:T(8,128)}, u32[]{:S(2)}, u32[]{:S(2)}) collective-permute-start(f32[172,8,128]{2,1,0:T(8,128)} %get-tuple-element.38), channel_id=1, source_target_pairs={{0,224},{32,0},{64,32},{96,64},{128,96},{160,128},{192,160},{224,1... | collective-permute-start | bytes 2113544 | tf_op jit(solution)/shard_map/ppermute | solution.py:851
  29.0 3.9 %collective-permute-start.5 = (f32[24,1024]{1,0:T(8,128)S(1)}, f32[24,1024]{1,0:T(8,128)S(1)}, u32[]{:S(2)}, u32[]{:S(2)}) collective-permute-start(f32[24,1024]{1,0:T(8,128)S(1)} %push.1.lists), channel_id=1, source_target_pairs={{0,224},{32,0},{64,32},{96,64},{128,96},{160,128},{192,160},{224,1... | collective-permute-start | bytes 294920 | tf_op jit(solution)/shard_map/ppermute | solution.py:856
  29.3 5.3 %collective-permute-start.4 = (f32[24,1024]{1,0:T(8,128)S(1)}, f32[24,1024]{1,0:T(8,128)S(1)}, u32[]{:S(2)}, u32[]{:S(2)}) collective-permute-start(f32[24,1024]{1,0:T(8,128)S(1)} %push.1.lists), channel_id=1, source_target_pairs={{0,32},{32,64},{64,96},{96,128},{128,160},{160,192},{192,224},{224... | collective-permute-start | bytes 294920 | tf_op jit(solution)/shard_map/ppermute | solution.py:855
  32.5 26.6 %copy-start = (f32[4,18,4,16,128]{4,3,2,1,0:T(8,128)}, f32[4,18,4,16,128]{4,3,2,1,0:T(8,128)S(1)}, u32[]{:S(2)}) copy-start(f32[4,18,4,16,128]{4,3,2,1,0:T(8,128)S(1)} %get-tuple-element.42.s_own) | copy-start | bytes 7077892
  45.3 5.2 %collective-permute-start.6 = (f32[19,8,128]{2,1,0:T(8,128)S(1)}, f32[19,8,128]{2,1,0:T(8,128)S(1)}, u32[]{:S(2)}, u32[]{:S(2)}) collective-permute-start(f32[19,8,128]{2,1,0:T(8,128)S(1)} %get-tuple-element.47), channel_id=1, source_target_pairs={{0,31},{1,0},{2,1},{3,2},{4,3},{5,4},{6,5},{7,6},{8,7},{9,8},{10,9... | collective-permute-start | bytes 233480 | tf_op jit(solution)/shard_map/ppermute | solution.py:894
  48.3 4.4 %collective-permute-start.7 = (f32[19,8,128]{2,1,0:T(8,128)S(1)}, f32[19,8,128]{2,1,0:T(8,128)S(1)}, u32[]{:S(2)}, u32[]{:S(2)}) collective-permute-start(f32[19,8,128]{2,1,0:T(8,128)S(1)} %get-tuple-element.48), channel_id=1, source_target_pairs={{0,1},{1,2},{2,3},{3,4},{4,5},{5,6},{6,7},{7,8},{8,9},{9,10},{10,1... | collective-permute-start | bytes 233480 | tf_op jit(solution)/shard_map/ppermute | solution.py:893
  52.7 6.3 %collective-permute-start.8 = (f32[48,8,128]{2,1,0:T(8,128)S(1)}, f32[48,8,128]{2,1,0:T(8,128)S(1)}, u32[]{:S(2)}, u32[]{:S(2)}) collective-permute-start(f32[48,8,128]{2,1,0:T(8,128)S(1)} %get-tuple-element.51.right_msg), channel_id=1, source_target_pairs={{0,32},{32,64},{64,96},{96,128},{128,160},{160,192},{192,224},{224... | collective-permute-start | bytes 589832 | tf_op jit(solution)/shard_map/ppermute | solution.py:906
  52.8 6.3 %collective-permute-start.9 = (f32[48,8,128]{2,1,0:T(8,128)S(1)}, f32[48,8,128]{2,1,0:T(8,128)S(1)}, u32[]{:S(2)}, u32[]{:S(2)}) collective-permute-start(f32[48,8,128]{2,1,0:T(8,128)S(1)} %get-tuple-element.52.left_msg), channel_id=1, source_target_pairs={{0,224},{32,0},{64,32},{96,64},{128,96},{160,128},{192,160},{224,1... | collective-permute-start | bytes 589832 | tf_op jit(solution)/shard_map/ppermute | solution.py:907
  62.5 17.7 %all-to-all-start.1 = ((f32[32,1,192]{2,1,0:T(1,128)}), f32[32,1,192]{2,1,0:T(1,128)S(1)}, u32[]{:S(2)}, u32[]{:S(2)}) async-start(f32[32,1,192]{2,1,0:T(1,128)} %get-tuple-element.57), calls=%async_computation.1 | async-start | bytes 65536 | tf_op jit(solution)/shard_map/all_to_all | solution.py:945
  71.6 1.7 %copy-start.1 = (f32[4,18,4,16,128]{4,3,2,1,0:T(8,128)S(1)}, f32[4,18,4,16,128]{4,3,2,1,0:T(8,128)}, u32[]{:S(2)}) copy-start(f32[4,18,4,16,128]{4,3,2,1,0:T(8,128)} %copy-done) | copy-start | bytes 7077892
  73.3 1.2 %copy-start.2 = (f32[19,6,16,128]{3,2,1,0:T(8,128)S(1)}, f32[19,6,16,128]{3,2,1,0:T(8,128)}, u32[]{:S(2)}) copy-start(f32[19,6,16,128]{3,2,1,0:T(8,128)} %get-tuple-element.56.a1) | copy-start | bytes 2801668
